TPU v7x, 128 devices: a whole 4x4x4 slice. The times are simulated.
128 devices in a mesh: lon: 16 (over y, x), lat: 8 (over z, core).
Axes of the slice: x: 4, y: 4, z: 4, core: 2. Of those that a mesh axis runs over, the one named last changes fastest.
Arguments:
- velocity_start: float32 [2, 1024, 8192], P(None, 'lat', 'lon'), may hold values from -1.5 to 1.5
- forcing: float32 [2, 1024, 8192], P(None, 'lat', 'lon'), may hold values from -1.8 to 1.8
- strength: float32 [1024, 8192], P('lat', 'lon'), may hold values from 1.5 to 3
- mobility: float32 [1024, 8192], P('lat', 'lon'), may hold values from 0.5 to 1
- plan: int32 [8, 64], P('lat', 'lon'), may hold values from -1 to 31, as said below
- stress_in: float32 [8, 32, 3, 128, 128], P('lat', 'lon'), may hold values from -4 to 4
Outputs:
- velocity: float32 [2, 1024, 8192], P(None, 'lat', 'lon')
- force: float32 [2, 1024, 8192], P(None, 'lat', 'lon')
- stress_out: float32 [8, 32, 3, 128, 128], P('lat', 'lon')
Inputs may be any that keep to these rules, and one draw needn't show every extreme that they name: plan[r, c] = o * 2 + s puts block (r, c) into slot s of the device at lon index o of the same lat row; -1 marks a block without ice. Every device of a lat row receives exactly 2 blocks, each slot once, and no device sends more than 1 block to one device.
All inputs are finite; a program needn't handle non-finite values.
Results may differ from a plain program's by a relative error of at most 0.00002.
Values sent between devices are 32-bit elements; how exact they have to be, the bound alone decides.
A program may use at most 128 MiB of HBM per device.

v0:
```python
import jax
import jax.numpy as jnp
import numpy as np
from jax import lax
from jax.sharding import PartitionSpec as P

NSUB = 4


STRESS_DAMPING = 4.0
MOMENTUM_DAMPING = 4.0
ELLIPSE_RATIO = 4.0
FLOOR_SQUARE = 0.0625
OCEAN_DRAG = 1.0
CORIOLIS = 0.3


def with_halo(value, sides, width, wrap):
    for axis, dim in sides:
        count, length = (lax.axis_size(axis), value.shape[dim])
        up = [(i, (i + 1) % count) for i in range(count if wrap else count - 1)]
        down = [(j, i) for i, j in up]
        last = lax.slice_in_dim(value, length - width, length, axis=dim)
        initial = lax.slice_in_dim(value, 0, width, axis=dim)
        before = lax.ppermute(last, axis, up)
        after = lax.ppermute(initial, axis, down)
        value = jnp.concatenate([before, value, after], axis=dim)
    return value


def interior(array, margin):
    return array[..., margin : array.shape[-2] - margin, margin : array.shape[-1] - margin]


def diff_x(array):
    return (array[..., 1:-1, 2:] - array[..., 1:-1, :-2]) * 0.5


def diff_y(array):
    return (array[..., 2:, 1:-1] - array[..., :-2, 1:-1]) * 0.5


def subcycle(fields, forcing_terms, ice_mask):
    velocity_x, velocity_y, stress_sum, stress_diff, stress_shear = fields
    start_x, start_y, pressure, mobile, push_x, push_y = forcing_terms
    grad_xx = diff_x(velocity_x)
    grad_xy = diff_y(velocity_x)
    grad_yx = diff_x(velocity_y)
    grad_yy = diff_y(velocity_y)
    divergence = grad_xx + grad_yy
    tension = grad_xx - grad_yy
    shearing = grad_xy + grad_yx
    deform_rate = jnp.sqrt(
        divergence * divergence
        + (tension * tension + shearing * shearing) / ELLIPSE_RATIO
        + FLOOR_SQUARE
    )
    strength_in = interior(pressure, 1)
    mask_in = interior(ice_mask, 1)
    new_sum = (
        mask_in
        * (
            STRESS_DAMPING * interior(stress_sum, 1)
            + strength_in * (divergence / deform_rate - 1.0)
        )
        / (1.0 + STRESS_DAMPING)
    )
    new_diff = (
        mask_in
        * (
            STRESS_DAMPING * interior(stress_diff, 1)
            + strength_in * tension / (ELLIPSE_RATIO * deform_rate)
        )
        / (1.0 + STRESS_DAMPING)
    )
    new_shear = (
        mask_in
        * (
            STRESS_DAMPING * interior(stress_shear, 1)
            + strength_in * shearing / (2.0 * ELLIPSE_RATIO * deform_rate)
        )
        / (1.0 + STRESS_DAMPING)
    )
    mask_core = interior(ice_mask, 2)
    force_x = mask_core * (diff_x(0.5 * (new_sum + new_diff)) + diff_y(new_shear))
    force_y = mask_core * (diff_x(new_shear) + diff_y(0.5 * (new_sum - new_diff)))
    mobile_core = interior(mobile, 2)
    old_x = interior(velocity_x, 2)
    old_y = interior(velocity_y, 2)
    damping = MOMENTUM_DAMPING + 1.0 + mobile_core * OCEAN_DRAG
    next_x = (
        mask_core
        * (
            MOMENTUM_DAMPING * old_x
            + interior(start_x, 2)
            + mobile_core * (force_x + interior(push_x, 2) + CORIOLIS * old_y)
        )
        / damping
    )
    next_y = (
        mask_core
        * (
            MOMENTUM_DAMPING * old_y
            + interior(start_y, 2)
            + mobile_core * (force_y + interior(push_y, 2) - CORIOLIS * old_x)
        )
        / damping
    )
    return (
        (next_x, next_y, interior(new_sum, 1), interior(new_diff, 1), interior(new_shear, 1)),
        (force_x, force_y),
    )


def select_rows(array, index, valid):
    taken = jnp.take(array, index, axis=0)
    return taken * valid.astype(taken.dtype).reshape((-1,) + (1,) * (taken.ndim - 1))


def from_blocks(blocks, rows_dev, cols_dev, block_side):
    field_count = blocks.shape[1]
    shaped = blocks.reshape(rows_dev, cols_dev, field_count, block_side, block_side)
    return shaped.transpose(2, 0, 3, 1, 4).reshape(
        field_count, rows_dev * block_side, cols_dev * block_side
    )


def windows(extended, cols_dev, block_side, halo_width):
    pieces = []
    for column_index in range(cols_dev):
        top_row = 0
        left_column = column_index * block_side
        pieces.append(
            extended[
                :,
                top_row : top_row + block_side + 2 * halo_width,
                left_column : left_column + block_side + 2 * halo_width,
            ]
        )
    return jnp.stack(pieces)


def clear_edges(extended, halo_width, here_lat, lat_count):
    row_ids = jnp.arange(extended.shape[1])
    dropped = (row_ids < halo_width) & (here_lat == 0) | (
        row_ids >= extended.shape[1] - halo_width
    ) & (here_lat == lat_count - 1)
    return extended * jnp.where(dropped, 0.0, 1.0).astype(extended.dtype)[:, None]


def spread_mask(nearby, row_sizes, column_sizes):
    widened = jnp.repeat(nearby, np.array(row_sizes), axis=0, total_repeat_length=sum(row_sizes))
    return jnp.repeat(
        widened, np.array(column_sizes), axis=1, total_repeat_length=sum(column_sizes)
    )


def fill_block(own_rims, halo_width, block_side):
    top_rows = own_rims[:, :, 0]
    bottom_rows = own_rims[:, :, 1]
    left_cells = jnp.swapaxes(own_rims[:, :, 2], -1, -2)
    right_cells = jnp.swapaxes(own_rims[:, :, 3], -1, -2)
    hollow = jnp.zeros(
        own_rims.shape[:2] + (block_side - 2 * halo_width, block_side - 2 * halo_width),
        own_rims.dtype,
    )
    middle = jnp.concatenate(
        [
            left_cells[..., halo_width : block_side - halo_width, :],
            hollow,
            right_cells[..., halo_width : block_side - halo_width, :],
        ],
        axis=-1,
    )
    return jnp.concatenate([top_rows, middle, bottom_rows], axis=-2)


def body(velocity_start, forcing, strength, mobility, plan, stress_in):
    rows_dev, cols_dev = plan.shape
    block_side = stress_in.shape[-1]
    slot_count = stress_in.shape[1]
    block_count = rows_dev * cols_dev
    lon_count = lax.axis_size("lon")
    lat_count = lax.axis_size("lat")
    capacity = (block_count + lon_count - 1) // lon_count
    here_lon = lax.axis_index("lon")
    here_lat = lax.axis_index("lat")
    outer_margin = 8
    halo_depth = 1
    halo_width = 2 * halo_depth
    plan_row = lax.all_gather(plan, "lon", axis=1, tiled=True)
    row_activity = (plan_row >= 0).astype(jnp.float32)
    activity_ext = with_halo(row_activity, (("lat", 0),), 1, False)
    activity_pad = jnp.concatenate(
        [activity_ext[:, -1:], activity_ext, activity_ext[:, :1]], axis=1
    )
    by_source = (
        plan_row.reshape(rows_dev, lon_count, cols_dev)
        .transpose(1, 0, 2)
        .reshape(lon_count, block_count)
    )
    has_ice = by_source >= 0
    target = jnp.where(has_ice, by_source // slot_count, -1)
    seat_index = jnp.where(has_ice, by_source % slot_count, -1)
    block_ids = jnp.arange(block_count, dtype=jnp.int32)
    peer_ids = jnp.arange(lon_count, dtype=jnp.int32)
    seat_ids = jnp.arange(capacity, dtype=jnp.int32)
    slot_ids = jnp.arange(slot_count, dtype=jnp.int32)
    earlier = block_ids[None, :] < block_ids[:, None]
    same_target = (target[:, :, None] == target[:, None, :]) & has_ice[:, None, :] & earlier[None]
    order_rank = jnp.sum(same_target.astype(jnp.int32), axis=-1)
    my_target = jnp.take(target, here_lon, axis=0)
    my_rank = jnp.take(order_rank, here_lon, axis=0)
    my_ice = jnp.take(has_ice, here_lon, axis=0)
    outgoing = (
        my_ice[None, None, :]
        & (my_target[None, None, :] == peer_ids[:, None, None])
        & (my_rank[None, None, :] == seat_ids[None, :, None])
    )
    send_index = jnp.sum(outgoing.astype(jnp.int32) * block_ids, axis=-1).reshape(-1)
    send_valid = jnp.any(outgoing, axis=-1).reshape(-1)
    home_index = jnp.where(my_ice, my_target * capacity + my_rank, 0)
    slot_holds = (
        has_ice[None] & (target[None] == here_lon) & (seat_index[None] == slot_ids[:, None, None])
    ).astype(jnp.int32)
    arrive_index = jnp.sum(
        slot_holds * (peer_ids[:, None] * capacity + order_rank)[None], axis=(1, 2)
    )
    holds_any = jnp.sum(slot_holds, axis=-1) > 0
    rank_of = jnp.sum(slot_holds * order_rank[None], axis=-1)
    leaving = holds_any.T[:, None, :] & (rank_of.T[:, None, :] == seat_ids[None, :, None])
    leave_index = jnp.sum(leaving.astype(jnp.int32) * slot_ids, axis=-1).reshape(-1)
    leave_valid = jnp.any(leaving, axis=-1).reshape(-1)
    slot_row = jnp.sum(slot_holds * (block_ids // cols_dev)[None, None, :], axis=(1, 2))
    slot_column = jnp.sum(
        slot_holds * (peer_ids[:, None] * cols_dev + block_ids % cols_dev)[None], axis=(1, 2)
    )
    const_tile = jnp.stack(
        [velocity_start[0], velocity_start[1], strength, mobility, forcing[0], forcing[1]]
    )
    const_ext = with_halo(const_tile, (("lat", 1), ("lon", 2)), outer_margin, True)
    const_ext = clear_edges(const_ext, outer_margin, here_lat, lat_count)
    const_windows = windows(const_ext, cols_dev, block_side, outer_margin)
    arrived = lax.all_to_all(
        select_rows(const_windows, send_index, send_valid),
        "lon",
        split_axis=0,
        concat_axis=0,
        tiled=True,
    )
    slot_consts = jnp.take(arrived, arrive_index, axis=0)

    def slot_mask(row_start, column_start):
        nearby = lax.dynamic_slice(activity_pad, (row_start, column_start), (3, 3))
        sizes = [outer_margin, block_side, outer_margin]
        return spread_mask(nearby, sizes, sizes)

    slot_masks = jax.vmap(slot_mask)(slot_row, slot_column)
    state_now = jnp.concatenate([interior(slot_consts[:, 0:2], outer_margin), stress_in[0]], axis=1)
    force_pair = None
    for group_index in range(NSUB // halo_depth):
        top_rows = state_now[..., :halo_width, :]
        bottom_rows = state_now[..., block_side - halo_width :, :]
        left_cells = jnp.swapaxes(state_now[..., :, :halo_width], -1, -2)
        right_cells = jnp.swapaxes(state_now[..., :, block_side - halo_width :], -1, -2)
        rims = jnp.stack([top_rows, bottom_rows, left_cells, right_cells], axis=2)
        refresh_returned = lax.all_to_all(
            select_rows(rims, leave_index, leave_valid),
            "lon",
            split_axis=0,
            concat_axis=0,
            tiled=True,
        )
        own_rims = select_rows(refresh_returned, home_index, my_ice)
        geo_tile = from_blocks(
            fill_block(own_rims, halo_width, block_side), rows_dev, cols_dev, block_side
        )
        extended = with_halo(geo_tile, (("lat", 1), ("lon", 2)), halo_width, True)
        extended = clear_edges(extended, halo_width, here_lat, lat_count)
        framed = windows(extended, cols_dev, block_side, halo_width)
        across_frame = jnp.stack(
            [framed[..., :halo_width, :], framed[..., block_side + halo_width :, :]], axis=2
        )
        beside_frame = jnp.stack(
            [
                jnp.swapaxes(
                    framed[..., halo_width : block_side + halo_width, :halo_width], -1, -2
                ),
                jnp.swapaxes(
                    framed[..., halo_width : block_side + halo_width, block_side + halo_width :],
                    -1,
                    -2,
                ),
            ],
            axis=2,
        )
        moved_across = lax.all_to_all(
            select_rows(across_frame, send_index, send_valid),
            "lon",
            split_axis=0,
            concat_axis=0,
            tiled=True,
        )
        moved_beside = lax.all_to_all(
            select_rows(beside_frame, send_index, send_valid),
            "lon",
            split_axis=0,
            concat_axis=0,
            tiled=True,
        )
        frame_rows = jnp.take(moved_across, arrive_index, axis=0)
        frame_sides = jnp.take(moved_beside, arrive_index, axis=0)
        middle = jnp.concatenate(
            [
                jnp.swapaxes(frame_sides[:, :, 0], -1, -2),
                state_now,
                jnp.swapaxes(frame_sides[:, :, 1], -1, -2),
            ],
            axis=-1,
        )
        extended_state = jnp.concatenate(
            [frame_rows[:, :, 0], middle, frame_rows[:, :, 1]], axis=-2
        )
        consts_now = interior(slot_consts, outer_margin - halo_width)
        masks_now = interior(slot_masks, outer_margin - halo_width)
        consts_step = interior(consts_now, 0)
        fields, force_pair = subcycle(
            tuple((extended_state[:, field_index] for field_index in range(5))),
            tuple((consts_step[:, field_index] for field_index in range(6))),
            interior(masks_now, 0),
        )
        extended_state = jnp.stack(fields, axis=1)
        state_now = extended_state
    results = jnp.concatenate([state_now[:, 0:2], jnp.stack(force_pair, axis=1)], axis=1)
    returned = lax.all_to_all(
        select_rows(results, leave_index, leave_valid),
        "lon",
        split_axis=0,
        concat_axis=0,
        tiled=True,
    )
    result_tile = from_blocks(
        select_rows(returned, home_index, my_ice), rows_dev, cols_dev, block_side
    )
    return (result_tile[0:2], result_tile[2:4], state_now[:, 2:5][None])


def solution(mesh):
    placed = (
        P(None, "lat", "lon"),
        P(None, "lat", "lon"),
        P("lat", "lon"),
        P("lat", "lon"),
        P("lat", "lon"),
        P("lat", "lon", None, None, None),
    )
    return jax.shard_map(
        body,
        mesh=mesh,
        in_specs=placed,
        out_specs=(P(None, "lat", "lon"), P(None, "lat", "lon"), P("lat", "lon", None, None, None)),
        check_vma=False,
    )
```

profile of v0, /device:TPU:96, one launch (start us, length us, event | category | flops | bytes accessed | tf_op | source)
XLA Modules:
  0.0 672.7 jit_solution(18413006784889373649)
XLA Ops:
  4.8 16.5 %all-reduce.2 = s32[64]{0:T(128)S(1)} all-reduce(s32[64]{0:T(128)S(1)} %bitcast_dynamic-update-slice_fusion.6), channel_id=1, replica_groups=mesh['lon'=16,'lat'=8] {'lon'}, use_global_device_ids=true, to_apply=%add.2 | all-reduce | flops 64 | bytes 512
  30.1 6.3 collective-permute-done.4
  37.8 6.6 gather_fusion.2
  44.4 12.0 %select_multiply_fusion = f32[16,6,144,144]{3,2,1,0:T(8,128)} fusion(f32[16,6,144,144]{3,2,1,0:T(8,128)} %gather_fusion.2, f32[16]{0:T(128)S(1)} %convert_element_type.63, pred[16]{0:T(512)(128)(4,1)S(1)} %compare_and_fusion.2), kind=kLoop, calls=%fused_computation.32 | loop fusion | flops 3981312 | bytes 15925328 | tf_op jit(solution)/shard_map/mul | solution.py:117
  56.4 6.9 %all-to-all-start = ((f32[16,6,144,144]{3,2,1,0:T(8,128)}), f32[16,6,144,144]{3,2,1,0:T(8,128)}, u32[]{:S(2)}, u32[]{:S(2)}) async-start(f32[16,6,144,144]{3,2,1,0:T(8,128)} %select_multiply_fusion), calls=%async_computation | async-start | bytes 28311552 | tf_op jit(solution)/shard_map/all_to_all | solution.py:244
  71.8 187.9 %all-to-all-done = f32[16,6,144,144]{3,2,1,0:T(8,128)} async-done(((f32[16,6,144,144]{3,2,1,0:T(8,128)}), f32[16,6,144,144]{3,2,1,0:T(8,128)}, u32[]{:S(2)}, u32[]{:S(2)}) %all-to-all-start) | async-done | bytes 7962656 | tf_op jit(solution)/shard_map/all_to_all | solution.py:244
  259.7 5.7 gather_fusion.3
  269.1 6.8 %all-to-all-start.1 = ((f32[16,5,4,2,128]{4,2,3,1,0:T(4,128)}), f32[16,5,4,2,128]{4,2,3,1,0:T(4,128)S(1)}, u32[]{:S(2)}, u32[]{:S(2)}) async-start(f32[16,5,4,2,128]{4,2,3,1,0:T(4,128)} %select_multiply_fusion.9), calls=%async_computation.1 | async-start | bytes 655360 | tf_op jit(solution)/shard_map/all_to_all | solution.py:267
  276.1 8.9 %all-to-all-done.1 = f32[16,5,4,2,128]{4,2,3,1,0:T(4,128)S(1)} async-done(((f32[16,5,4,2,128]{4,2,3,1,0:T(4,128)}), f32[16,5,4,2,128]{4,2,3,1,0:T(4,128)S(1)}, u32[]{:S(2)}, u32[]{:S(2)}) %all-to-all-start.1) | async-done | bytes 327712 | tf_op jit(solution)/shard_map/all_to_all | solution.py:267
  297.4 5.2 collective-permute-start.9
  304.1 5.0 collective-permute-done.8
  315.3 6.9 %all-to-all-start.3 = ((f32[16,5,2,2,128]{4,3,2,1,0:T(2,128)}), f32[16,5,2,2,128]{4,3,2,1,0:T(2,128)S(1)}, u32[]{:S(2)}, u32[]{:S(2)}) async-start(f32[16,5,2,2,128]{4,3,2,1,0:T(2,128)} %select_multiply_fusion.13), calls=%async_computation.3 | async-start | bytes 327680 | tf_op jit(solution)/shard_map/all_to_all | solution.py:304
  325.1 5.3 all-to-all-done.3
  352.7 11.9 %all_to_all.70 = f32[16,5,4,2,128]{4,2,3,1,0:T(4,128)S(1)} all-to-all(f32[16,5,4,2,128]{4,2,3,1,0:T(4,128)S(1)} %select_multiply_fusion.7), channel_id=1, replica_groups=mesh['lon'=16,'lat'=8] {'lon'}, dimensions={0} | all-to-all | bytes 655360 | tf_op jit(solution)/shard_map/all_to_all | solution.py:267
  380.9 6.8 %collective-permute-done.12 = f32[5,132,2]{2,1,0:T(8,128)S(1)} collective-permute-done((f32[5,132,2]{2,1,0:T(8,128)S(1)}, f32[5,132,2]{2,1,0:T(8,128)S(1)}, u32[]{:S(2)}, u32[]{:S(2)}) %collective-permute-start.12) | collective-permute-done | bytes 5312 | tf_op jit(solution)/shard_map/ppermute | solution.py:25
  393.8 7.2 %all-to-all-start.6 = ((f32[16,5,2,2,128]{4,3,2,1,0:T(2,128)}), f32[16,5,2,2,128]{4,3,2,1,0:T(2,128)S(1)}, u32[]{:S(2)}, u32[]{:S(2)}) async-start(f32[16,5,2,2,128]{4,3,2,1,0:T(2,128)} %select_multiply_fusion.12), calls=%async_computation.6 | async-start | bytes 327680 | tf_op jit(solution)/shard_map/all_to_all | solution.py:304
  403.9 5.8 all-to-all-done.6
  418.1 5.1 all-to-all-done.5
  433.0 12.0 %all_to_all.71 = f32[16,5,4,2,128]{4,2,3,1,0:T(4,128)S(1)} all-to-all(f32[16,5,4,2,128]{4,2,3,1,0:T(4,128)S(1)} %select_multiply_fusion.5), channel_id=1, replica_groups=mesh['lon'=16,'lat'=8] {'lon'}, dimensions={0} | all-to-all | bytes 655360 | tf_op jit(solution)/shard_map/all_to_all | solution.py:267
  456.2 5.0 collective-permute-start.17
  461.2 6.0 collective-permute-done.16
  473.5 7.2 %all-to-all-start.9 = ((f32[16,5,2,2,128]{4,3,2,1,0:T(2,128)}), f32[16,5,2,2,128]{4,3,2,1,0:T(2,128)S(1)}, u32[]{:S(2)}, u32[]{:S(2)}) async-start(f32[16,5,2,2,128]{4,3,2,1,0:T(2,128)} %select_multiply_fusion.11), calls=%async_computation.9 | async-start | bytes 327680 | tf_op jit(solution)/shard_map/all_to_all | solution.py:304
  483.6 5.3 all-to-all-done.9
  497.3 5.8 all-to-all-done.8
  512.9 12.5 %all_to_all.72 = f32[16,5,4,2,128]{4,2,3,1,0:T(4,128)S(1)} all-to-all(f32[16,5,4,2,128]{4,2,3,1,0:T(4,128)S(1)} %select_multiply_fusion.3), channel_id=1, replica_groups=mesh['lon'=16,'lat'=8] {'lon'}, dimensions={0} | all-to-all | bytes 655360 | tf_op jit(solution)/shard_map/all_to_all | solution.py:267
  536.9 5.0 collective-permute-start.21
  542.4 5.4 collective-permute-done.20
  553.5 7.2 %all-to-all-start.12 = ((f32[16,5,2,2,128]{4,3,2,1,0:T(2,128)}), f32[16,5,2,2,128]{4,3,2,1,0:T(2,128)S(1)}, u32[]{:S(2)}, u32[]{:S(2)}) async-start(f32[16,5,2,2,128]{4,3,2,1,0:T(2,128)} %select_multiply_fusion.10), calls=%async_computation.12 | async-start | bytes 327680 | tf_op jit(solution)/shard_map/all_to_all | solution.py:304
  563.6 5.3 all-to-all-done.12
  577.4 5.8 all-to-all-done.11
  593.3 5.1 select_multiply_fusion.1
  604.0 62.7 %all-to-all-done.13 = f32[16,4,128,128]{3,2,1,0:T(8,128)} async-done(((f32[16,4,128,128]{3,2,1,0:T(8,128)}), f32[16,4,128,128]{3,2,1,0:T(8,128)}, u32[]{:S(2)}, u32[]{:S(2)}) %all-to-all-start.13) | async-done | bytes 4194336 | tf_op jit(solution)/shard_map/all_to_all | solution.py:335
  (443 shorter events, 204.7 us)
Async XLA Ops:
  1.7 22.7 %collective-permute-start.2 = (f32[6,8,512]{2,1,0:T(8,128)S(1)}, f32[6,8,512]{2,1,0:T(8,128)S(1)}, u32[]{:S(2)}, u32[]{:S(2)}) collective-permute-start(f32[6,8,512]{2,1,0:T(8,128)S(1)} %get-tuple-element.220), channel_id=1, source_target_pairs={{0,1},{1,2},{2,3},{3,4},{4,5},{5,6},{6,7},{7,0},{8,9},{9,10},{10,1... | collective-permute-start | bytes 294920 | tf_op jit(solution)/shard_map/ppermute | solution.py:25
  1.7 22.7 %collective-permute-start.3 = (f32[6,8,512]{2,1,0:T(8,128)S(1)}, f32[6,8,512]{2,1,0:T(8,128)S(1)}, u32[]{:S(2)}, u32[]{:S(2)}) collective-permute-start(f32[6,8,512]{2,1,0:T(8,128)S(1)} %get-tuple-element.221), channel_id=1, source_target_pairs={{1,0},{2,1},{3,2},{4,3},{5,4},{6,5},{7,6},{0,7},{9,8},{10,9},{11,1... | collective-permute-start | bytes 294920 | tf_op jit(solution)/shard_map/ppermute | solution.py:26
  24.6 11.7 %collective-permute-start.4 = (f32[6,144,8]{2,1,0:T(8,128)S(1)}, f32[6,144,8]{2,1,0:T(8,128)S(1)}, u32[]{:S(2)}, u32[]{:S(2)}) collective-permute-start(f32[6,144,8]{2,1,0:T(8,128)S(1)} %get-tuple-element.202), channel_id=1, source_target_pairs={{0,8},{8,16},{16,24},{24,32},{32,40},{40,48},{48,56},{56,64},{64,7... | collective-permute-start | bytes 82952 | tf_op jit(solution)/shard_map/ppermute | solution.py:25
  25.3 11.0 %collective-permute-start.5 = (f32[6,144,8]{2,1,0:T(8,128)S(1)}, f32[6,144,8]{2,1,0:T(8,128)S(1)}, u32[]{:S(2)}, u32[]{:S(2)}) collective-permute-start(f32[6,144,8]{2,1,0:T(8,128)S(1)} %get-tuple-element.203), channel_id=1, source_target_pairs={{8,0},{16,8},{24,16},{32,24},{40,32},{48,40},{56,48},{64,56},{72,6... | collective-permute-start | bytes 82952 | tf_op jit(solution)/shard_map/ppermute | solution.py:26
  56.4 203.3 %all-to-all-start = ((f32[16,6,144,144]{3,2,1,0:T(8,128)}), f32[16,6,144,144]{3,2,1,0:T(8,128)}, u32[]{:S(2)}, u32[]{:S(2)}) async-start(f32[16,6,144,144]{3,2,1,0:T(8,128)} %select_multiply_fusion), calls=%async_computation | async-start | bytes 28311552 | tf_op jit(solution)/shard_map/all_to_all | solution.py:244
  63.4 8.4 %collective-permute-start = (f32[1,64]{1,0:T(1,128)S(1)}, f32[1,64]{1,0:T(1,128)S(1)}, u32[]{:S(2)}, u32[]{:S(2)}) collective-permute-start(f32[1,64]{1,0:T(1,128)S(1)} %fusion.145), channel_id=1, source_target_pairs={{0,1},{1,2},{2,3},{3,4},{4,5},{5,6},{6,7},{8,9},{9,10},{10,11},{11... | collective-permute-start | bytes 776 | tf_op jit(solution)/shard_map/ppermute | solution.py:25
  65.3 6.4 collective-permute-start.1
  269.1 15.9 %all-to-all-start.1 = ((f32[16,5,4,2,128]{4,2,3,1,0:T(4,128)}), f32[16,5,4,2,128]{4,2,3,1,0:T(4,128)S(1)}, u32[]{:S(2)}, u32[]{:S(2)}) async-start(f32[16,5,4,2,128]{4,2,3,1,0:T(4,128)} %select_multiply_fusion.9), calls=%async_computation.1 | async-start | bytes 655360 | tf_op jit(solution)/shard_map/all_to_all | solution.py:267
  290.1 6.5 collective-permute-start.6
  290.1 6.5 collective-permute-start.7
  296.8 12.3 %collective-permute-start.8 = (f32[5,132,2]{2,1,0:T(8,128)S(1)}, f32[5,132,2]{2,1,0:T(8,128)S(1)}, u32[]{:S(2)}, u32[]{:S(2)}) collective-permute-start(f32[5,132,2]{2,1,0:T(8,128)S(1)} %get-tuple-element.248), channel_id=1, source_target_pairs={{0,8},{8,16},{16,24},{24,32},{32,40},{40,48},{48,56},{56,64},{64,7... | collective-permute-start | bytes 15848 | tf_op jit(solution)/shard_map/ppermute | solution.py:25
  297.4 11.7 %collective-permute-start.9 = (f32[5,132,2]{2,1,0:T(8,128)S(1)}, f32[5,132,2]{2,1,0:T(8,128)S(1)}, u32[]{:S(2)}, u32[]{:S(2)}) collective-permute-start(f32[5,132,2]{2,1,0:T(8,128)S(1)} %get-tuple-element.249), channel_id=1, source_target_pairs={{8,0},{16,8},{24,16},{32,24},{40,32},{48,40},{56,48},{64,56},{72,6... | collective-permute-start | bytes 15848 | tf_op jit(solution)/shard_map/ppermute | solution.py:26
  315.3 15.1 %all-to-all-start.3 = ((f32[16,5,2,2,128]{4,3,2,1,0:T(2,128)}), f32[16,5,2,2,128]{4,3,2,1,0:T(2,128)S(1)}, u32[]{:S(2)}, u32[]{:S(2)}) async-start(f32[16,5,2,2,128]{4,3,2,1,0:T(2,128)} %select_multiply_fusion.13), calls=%async_computation.3 | async-start | bytes 327680 | tf_op jit(solution)/shard_map/all_to_all | solution.py:304
  330.4 12.6 %all-to-all-start.2 = ((f32[16,5,2,2,132]{4,3,2,1,0:T(2,128)}), f32[16,5,2,2,132]{4,3,2,1,0:T(2,128)S(1)}, u32[]{:S(2)}, u32[]{:S(2)}) async-start(f32[16,5,2,2,132]{4,3,2,1,0:T(2,128)} %select_multiply_fusion.8), calls=%async_computation.2 | async-start | bytes 655360 | tf_op jit(solution)/shard_map/all_to_all | solution.py:297
  371.9 3.2 collective-permute-start.10
  375.3 12.3 %collective-permute-start.12 = (f32[5,132,2]{2,1,0:T(8,128)S(1)}, f32[5,132,2]{2,1,0:T(8,128)S(1)}, u32[]{:S(2)}, u32[]{:S(2)}) collective-permute-start(f32[5,132,2]{2,1,0:T(8,128)S(1)} %get-tuple-element.246), channel_id=1, source_target_pairs={{0,8},{8,16},{16,24},{24,32},{32,40},{40,48},{48,56},{56,64},{64,7... | collective-permute-start | bytes 15848 | tf_op jit(solution)/shard_map/ppermute | solution.py:25
  375.9 11.7 %collective-permute-start.13 = (f32[5,132,2]{2,1,0:T(8,128)S(1)}, f32[5,132,2]{2,1,0:T(8,128)S(1)}, u32[]{:S(2)}, u32[]{:S(2)}) collective-permute-start(f32[5,132,2]{2,1,0:T(8,128)S(1)} %get-tuple-element.247), channel_id=1, source_target_pairs={{8,0},{16,8},{24,16},{32,24},{40,32},{48,40},{56,48},{64,56},{72,6... | collective-permute-start | bytes 15848 | tf_op jit(solution)/shard_map/ppermute | solution.py:26
  393.8 15.8 %all-to-all-start.6 = ((f32[16,5,2,2,128]{4,3,2,1,0:T(2,128)}), f32[16,5,2,2,128]{4,3,2,1,0:T(2,128)S(1)}, u32[]{:S(2)}, u32[]{:S(2)}) async-start(f32[16,5,2,2,128]{4,3,2,1,0:T(2,128)} %select_multiply_fusion.12), calls=%async_computation.6 | async-start | bytes 327680 | tf_op jit(solution)/shard_map/all_to_all | solution.py:304
  409.6 13.6 %all-to-all-start.5 = ((f32[16,5,2,2,132]{4,3,2,1,0:T(2,128)}), f32[16,5,2,2,132]{4,3,2,1,0:T(2,128)S(1)}, u32[]{:S(2)}, u32[]{:S(2)}) async-start(f32[16,5,2,2,132]{4,3,2,1,0:T(2,128)} %select_multiply_fusion.6), calls=%async_computation.5 | async-start | bytes 655360 | tf_op jit(solution)/shard_map/all_to_all | solution.py:297
  452.2 3.2 collective-permute-start.14
  452.2 3.2 collective-permute-start.15
  455.6 11.6 %collective-permute-start.16 = (f32[5,132,2]{2,1,0:T(8,128)S(1)}, f32[5,132,2]{2,1,0:T(8,128)S(1)}, u32[]{:S(2)}, u32[]{:S(2)}) collective-permute-start(f32[5,132,2]{2,1,0:T(8,128)S(1)} %get-tuple-element.244), channel_id=1, source_target_pairs={{0,8},{8,16},{16,24},{24,32},{32,40},{40,48},{48,56},{56,64},{64,7... | collective-permute-start | bytes 15848 | tf_op jit(solution)/shard_map/ppermute | solution.py:25
  456.2 11.0 %collective-permute-start.17 = (f32[5,132,2]{2,1,0:T(8,128)S(1)}, f32[5,132,2]{2,1,0:T(8,128)S(1)}, u32[]{:S(2)}, u32[]{:S(2)}) collective-permute-start(f32[5,132,2]{2,1,0:T(8,128)S(1)} %get-tuple-element.245), channel_id=1, source_target_pairs={{8,0},{16,8},{24,16},{32,24},{40,32},{48,40},{56,48},{64,56},{72,6... | collective-permute-start | bytes 15848 | tf_op jit(solution)/shard_map/ppermute | solution.py:26
  473.5 15.4 %all-to-all-start.9 = ((f32[16,5,2,2,128]{4,3,2,1,0:T(2,128)}), f32[16,5,2,2,128]{4,3,2,1,0:T(2,128)S(1)}, u32[]{:S(2)}, u32[]{:S(2)}) async-start(f32[16,5,2,2,128]{4,3,2,1,0:T(2,128)} %select_multiply_fusion.11), calls=%async_computation.9 | async-start | bytes 327680 | tf_op jit(solution)/shard_map/all_to_all | solution.py:304
  488.8 14.3 %all-to-all-start.8 = ((f32[16,5,2,2,132]{4,3,2,1,0:T(2,128)}), f32[16,5,2,2,132]{4,3,2,1,0:T(2,128)S(1)}, u32[]{:S(2)}, u32[]{:S(2)}) async-start(f32[16,5,2,2,132]{4,3,2,1,0:T(2,128)} %select_multiply_fusion.4), calls=%async_computation.8 | async-start | bytes 655360 | tf_op jit(solution)/shard_map/all_to_all | solution.py:297
  532.6 3.2 collective-permute-start.18
  532.6 3.4 collective-permute-start.19
  536.2 11.6 %collective-permute-start.20 = (f32[5,132,2]{2,1,0:T(8,128)S(1)}, f32[5,132,2]{2,1,0:T(8,128)S(1)}, u32[]{:S(2)}, u32[]{:S(2)}) collective-permute-start(f32[5,132,2]{2,1,0:T(8,128)S(1)} %get-tuple-element.242), channel_id=1, source_target_pairs={{0,8},{8,16},{16,24},{24,32},{32,40},{40,48},{48,56},{56,64},{64,7... | collective-permute-start | bytes 15848 | tf_op jit(solution)/shard_map/ppermute | solution.py:25
  536.9 11.1 %collective-permute-start.21 = (f32[5,132,2]{2,1,0:T(8,128)S(1)}, f32[5,132,2]{2,1,0:T(8,128)S(1)}, u32[]{:S(2)}, u32[]{:S(2)}) collective-permute-start(f32[5,132,2]{2,1,0:T(8,128)S(1)} %get-tuple-element.243), channel_id=1, source_target_pairs={{8,0},{16,8},{24,16},{32,24},{40,32},{48,40},{56,48},{64,56},{72,6... | collective-permute-start | bytes 15848 | tf_op jit(solution)/shard_map/ppermute | solution.py:26
  553.5 15.4 %all-to-all-start.12 = ((f32[16,5,2,2,128]{4,3,2,1,0:T(2,128)}), f32[16,5,2,2,128]{4,3,2,1,0:T(2,128)S(1)}, u32[]{:S(2)}, u32[]{:S(2)}) async-start(f32[16,5,2,2,128]{4,3,2,1,0:T(2,128)} %select_multiply_fusion.10), calls=%async_computation.12 | async-start | bytes 327680 | tf_op jit(solution)/shard_map/all_to_all | solution.py:304
  568.9 14.3 %all-to-all-start.11 = ((f32[16,5,2,2,132]{4,3,2,1,0:T(2,128)}), f32[16,5,2,2,132]{4,3,2,1,0:T(2,128)S(1)}, u32[]{:S(2)}, u32[]{:S(2)}) async-start(f32[16,5,2,2,132]{4,3,2,1,0:T(2,128)} %select_multiply_fusion.2), calls=%async_computation.11 | async-start | bytes 655360 | tf_op jit(solution)/shard_map/all_to_all | solution.py:297
  598.4 68.3 %all-to-all-start.13 = ((f32[16,4,128,128]{3,2,1,0:T(8,128)}), f32[16,4,128,128]{3,2,1,0:T(8,128)}, u32[]{:S(2)}, u32[]{:S(2)}) async-start(f32[16,4,128,128]{3,2,1,0:T(8,128)} %select_multiply_fusion.1), calls=%async_computation.13 | async-start | bytes 8388608 | tf_op jit(solution)/shard_map/all_to_all | solution.py:335
  (63 other events, 3174.3 us)
where the time goes:
time: 684 us; the launch traced here: 673 us
  waiting for transfers between devices  336 us (49%)
  starting transfers between devices  103 us (15%)
  local copies, waits for them, and re-layouts  90.5 us (13%)
  other arithmetic  86.1 us (13%)
  blocking collectives  52.9 us (8%)
    all_to_all x1, waiting for transfers between devices, body(): lax.all_to_all(select_rows(const_windows, send_index, send_valid), 'lon',...  188 us
    all_to_all x1, waiting for transfers between devices, body(): lax.all_to_all(select_rows(results, leave_index, leave_valid), 'lon', spl...  62.7 us
    ppermute x11, starting transfers between devices, with_halo(): after = lax.ppermute(initial, axis, down)  37.2 us
    all_to_all x3, blocking collectives, body(): lax.all_to_all(select_rows(rims, leave_index, leave_valid), 'lon', split_...  36.3 us
    ppermute x11, waiting for transfers between devices, with_halo(): before = lax.ppermute(last, axis, up)  33.9 us
    gather x19, local copies, waits for them, and re-layouts, select_rows(): taken = jnp.take(array, index, axis=0)  28.6 us
    all_to_all x4, starting transfers between devices, body(): lax.all_to_all(select_rows(beside_frame, send_index, send_valid), 'lon',...  28.4 us
    mul x18, other arithmetic, select_rows(): taken * valid.astype(taken.dtype).reshape((-1,) + (1,) * (taken.ndim - 1))  26.7 us
  transfers between devices with their start and end apart: 33, of which 21 were waited for; matrix products, arithmetic and copies ran while one was open for 7% of the time, Pallas kernels for 0%

commit v1 on v0

v1 whole, which is shorter than its diff:
```python
import functools

import jax
import jax.numpy as jnp
from jax import lax
from jax.experimental import pallas as pl
from jax.experimental.pallas import tpu as pltpu
from jax.sharding import PartitionSpec as P

NSUB = 4
LANES = 128
HALO = 8
TOP = 16
MESH = pl.DeviceIdType.MESH


def kernel(
    n_lon, n_lat,
    plan_ref, vel_ref, frc_ref, str_ref, mob_ref, sig_ref,
    o_vel, o_frc, o_sig,
    cst, edge_l, edge_r, halo_r, halo_l,
    plan_own, plan_all, plan_sm, inv_own, inv_sm,
    part, pack, sig, uv, coef, inc, back, home,
    loc_sem, one_sem, p1_s, p1_r, pl_s, pl_r, x_s, x_r, y_s, y_r,
    p2_s, p2_r, h_s, h_r, r1_s, r1_r, r2_s, r2_r,
):
    me = lax.axis_index("lon")
    lat = lax.axis_index("lat")
    right, left = lax.rem(me + 1, n_lon), lax.rem(me + n_lon - 1, n_lon)
    below, above = lax.rem(lat + 1, n_lat), lax.rem(lat + n_lat - 1, n_lat)
    side = LANES
    cols = plan_ref.shape[1]
    slots = sig_ref.shape[1]
    piece = side // n_lon
    tiles = (side + 2 * HALO) // 8
    lane1 = lax.broadcasted_iota(jnp.int32, (1, LANES), 1)
    lane = lax.broadcasted_iota(jnp.int32, (1, 1, LANES), 2)

    def to(src, dst, ss, rs, **where):
        return pltpu.make_async_remote_copy(
            src_ref=src, dst_ref=dst, send_sem=ss, recv_sem=rs,
            device_id=where, device_id_type=MESH,
        )

    def peers(fn):
        def step(k, carry):
            fn(lax.rem(me + k, n_lon))
            return carry
        lax.fori_loop(1, n_lon, step, 0)

    copies = []
    for j in range(cols):
        own = (pl.ds(TOP, side), slice(None))
        src_cols = pl.ds(j * LANES, LANES)
        copies += [
            (vel_ref.at[:, :, src_cols], cst.at[(pl.ds(0, 2), j) + own]),
            (frc_ref.at[:, :, src_cols], cst.at[(pl.ds(2, 2), j) + own]),
            (str_ref.at[:, src_cols], cst.at[(4, j) + own]),
            (mob_ref.at[:, src_cols], cst.at[(5, j) + own]),
        ]
    copies = [pltpu.make_async_copy(s, d, loc_sem.at[i]) for i, (s, d) in enumerate(copies)]
    for c in copies:
        c.start()
    row = jnp.full((1, LANES), -1, jnp.int32)
    for j in range(cols):
        row = jnp.where(lane1 == j, plan_ref[0, j], row)
        active = jnp.where(plan_ref[0, j] >= 0, 1.0, 0.0)
        cst[6, j, pl.ds(TOP, side), :] = jnp.full((side, LANES), active, jnp.float32)
    plan_own[...] = row

    barrier = pltpu.get_barrier_semaphore()
    peers(lambda d: pl.semaphore_signal(barrier, inc=1, device_id={"lon": d}, device_id_type=MESH))
    for other in (above, below):
        pl.semaphore_signal(barrier, inc=1, device_id={"lat": other}, device_id_type=MESH)
    pl.semaphore_wait(barrier, n_lon + 1)

    def stage1(d, sender):
        return to(
            sig_ref.at[0, :, :, pl.ds(d * piece, piece), :],
            part.at[pl.ds(sender * slots, slots)],
            p1_s.at[d], p1_r.at[sender], lon=d,
        )

    def planmsg(d, sender):
        return to(plan_own, plan_all.at[sender], pl_s.at[d], pl_r.at[sender], lon=d)

    peers(lambda d: planmsg(d, me).start())
    peers(lambda d: stage1(d, me).start())
    self1 = pltpu.make_async_copy(
        sig_ref.at[0, :, :, pl.ds(me * piece, piece), :],
        part.at[pl.ds(me * slots, slots)], one_sem.at[0],
    )
    self1.start()
    self_plan = pltpu.make_async_copy(plan_own, plan_all.at[me], one_sem.at[1])
    self_plan.start()

    for c in copies:
        c.wait()
    own_rows = pl.ds(TOP, side)
    pl_left = jnp.zeros((side, LANES), jnp.float32)
    pl_right = jnp.zeros((side, LANES), jnp.float32)
    for f in range(7):
        first, last = cst[f, 0, own_rows, :], cst[f, cols - 1, own_rows, :]
        if f:
            first = pltpu.roll(first, HALO * f, 1)
            last = pltpu.roll(last, LANES - HALO * f, 1)
        pl_left = jnp.where((lane1 >= HALO * f) & (lane1 < HALO * (f + 1)), first, pl_left)
        pl_right = jnp.where(
            (lane1 >= LANES - HALO * (f + 1)) & (lane1 < LANES - HALO * f), last, pl_right
        )
    edge_l[...] = pl_left
    edge_r[...] = pl_right
    x_copies = [
        to(edge_l, halo_r, x_s.at[0], x_r.at[0], lon=left),
        to(edge_r, halo_l, x_s.at[1], x_r.at[1], lon=right),
    ]
    for c in x_copies:
        c.start()
    for c in x_copies:
        c.wait_recv()
    from_r, from_l = halo_r[...], halo_l[...]
    for f in range(7):
        a, b = from_r, from_l
        if f:
            a = pltpu.roll(a, LANES - HALO * f, 1)
            b = pltpu.roll(b, HALO * f, 1)
        cst[f, cols, own_rows, :] = jnp.where(
            lane1 < HALO, a, jnp.where(lane1 >= LANES - HALO, b, 0.0)
        )
    y_copies = [
        to(cst.at[:, :, pl.ds(TOP, HALO), :], cst.at[:, :, pl.ds(TOP + side, HALO), :],
           y_s.at[0], y_r.at[0], lat=above),
        to(cst.at[:, :, pl.ds(TOP + side - HALO, HALO), :], cst.at[:, :, pl.ds(TOP - HALO, HALO), :],
           y_s.at[1], y_r.at[1], lat=below),
    ]
    for c in y_copies:
        c.start()

    peers(lambda d: planmsg(d, d).wait_recv())
    self_plan.wait()
    plan_copy = pltpu.make_async_copy(plan_all, plan_sm, one_sem.at[2])
    plan_copy.start()
    plan_copy.wait()

    peers(lambda d: stage1(d, d).wait_recv())
    self1.wait()

    def seat(d, j):
        return part[jnp.maximum(plan_sm[d, 0, j], 0)]

    def fill(d):
        for j in range(cols):
            pack[d, :, j] = seat(d, j)
        pack[d, :, cols] = jnp.where(
            lane < LANES // 2,
            seat(lax.rem(d + 1, n_lon), 0),
            seat(lax.rem(d + n_lon - 1, n_lon), cols - 1),
        )

    def stage2(d, sender):
        return to(
            pack.at[d], sig.at[:, :, pl.ds(TOP + sender * piece, piece), :],
            p2_s.at[d], p2_r.at[sender], lon=d,
        )

    def send2(d):
        fill(d)
        stage2(d, me).start()

    peers(send2)
    fill(me)
    self2 = pltpu.make_async_copy(
        pack.at[me], sig.at[:, :, pl.ds(TOP + me * piece, piece), :], one_sem.at[3]
    )
    self2.start()

    def invert(d, inv):
        for j in range(cols):
            inv = jnp.where(lane1 == plan_sm[d, 0, j], d * cols + j, inv)
        return inv
    inv_own[...] = lax.fori_loop(0, n_lon, invert, jnp.zeros((1, LANES), jnp.int32))
    inv_copy = pltpu.make_async_copy(inv_own, inv_sm, one_sem.at[4])
    inv_copy.start()

    for c in y_copies:
        c.wait_recv()

    def prepare(t, carry):
        rows = pl.ds(pl.multiple_of(HALO + 8 * t, 8), 8)
        outside = ((t == 0) & (lat == 0)) | ((t == tiles - 1) & (lat == n_lat - 1))
        mask = cst[6, :, rows, :] * jnp.where(outside, 0.0, 1.0)
        mob = cst[5, :, rows, :]
        ratio = mask / (5.0 + mob)
        push = ratio * mob
        sx, sy = cst[0, :, rows, :], cst[1, :, rows, :]
        uv[0, :, rows, :] = mask * sx
        uv[1, :, rows, :] = mask * sy
        coef[0, :, rows, :] = 0.2 * mask * cst[4, :, rows, :]
        coef[1, :, rows, :] = 4.0 * ratio
        coef[2, :, rows, :] = push
        coef[3, :, rows, :] = ratio * sx + push * cst[2, :, rows, :]
        coef[4, :, rows, :] = ratio * sy + push * cst[3, :, rows, :]
        coef[5, :, rows, :] = mask
        return carry

    lax.fori_loop(0, tiles, prepare, 0)

    def east(x):
        r = pltpu.roll(x, LANES - 1, 2)
        return jnp.where(lane == LANES - 1, jnp.concatenate([r[1:], r[:1]], 0), r)

    def west(x):
        r = pltpu.roll(x, 1, 2)
        return jnp.where(lane == 0, jnp.concatenate([r[-1:], r[:-1]], 0), r)

    def diff_x(x):
        return east(x) - west(x)

    def diff_y(ref, f, base):
        return ref[f, :, pl.ds(base + 1, 8), :] - ref[f, :, pl.ds(base - 1, 8), :]

    def increments(base, rows):
        u, v = uv[0, :, rows, :], uv[1, :, rows, :]
        ux, vx = diff_x(u), diff_x(v)
        uy, vy = diff_y(uv, 0, base), diff_y(uv, 1, base)
        div, ten, shr = ux + vy, ux - vy, uy + vx
        a = coef[0, :, rows, :]
        ar = a * lax.rsqrt(div * div + 0.25 * (ten * ten + shr * shr) + 0.25)
        ten4 = 0.25 * ten
        return ar * (div + ten4) - a, ar * (div - ten4) - a, ar * (0.25 * shr)

    def loop(lo, hi, fn):
        def step(t, carry):
            base = pl.multiple_of(HALO + 8 * t, 8)
            fn(base, pl.ds(base, 8))
            return carry
        lax.fori_loop(lo, hi, step, 0)

    def first_increments(base, rows):
        for f, value in enumerate(increments(base, rows)):
            inc[f, :, rows, :] = value

    loop(0, tiles, first_increments)

    def arrived2(sender):
        stage2(sender, sender).wait_recv()

    for sender in range(n_lon):
        @pl.when(me != sender)
        def _(sender=sender):
            arrived2(sender)

        @pl.when(me == sender)
        def _():
            self2.wait()

        if sender == 0:
            up = to(sig.at[:, :, pl.ds(TOP, HALO), :], sig.at[:, :, pl.ds(TOP + side, HALO), :],
                    h_s.at[0], h_r.at[0], lat=above)
            up.start()
    down = to(sig.at[:, :, pl.ds(TOP + side - HALO, HALO), :], sig.at[:, :, pl.ds(TOP - HALO, HALO), :],
              h_s.at[1], h_r.at[1], lat=below)
    down.start()
    for c in (up, down):
        c.wait()

    def stress_first(base, rows):
        w = 0.8 * coef[5, :, rows, :]
        s1, s2, s3 = (sig[f, :, rows, :] for f in range(3))
        sig[0, :, rows, :] = w * (s1 + s2) + inc[0, :, rows, :]
        sig[1, :, rows, :] = w * (s1 - s2) + inc[1, :, rows, :]
        sig[2, :, rows, :] = (w + w) * s3 + inc[2, :, rows, :]

    def stress_next(base, rows):
        for f, value in enumerate(increments(base, rows)):
            sig[f, :, rows, :] = 0.8 * sig[f, :, rows, :] + value

    def momentum(base, rows, emit):
        fx = 0.25 * (diff_x(sig[0, :, rows, :]) + diff_y(sig, 2, base))
        fy = 0.25 * (diff_x(sig[2, :, rows, :]) + diff_y(sig, 1, base))
        u, v = uv[0, :, rows, :], uv[1, :, rows, :]
        keep, push = coef[1, :, rows, :], coef[2, :, rows, :]
        un = keep * u + coef[3, :, rows, :] + push * (fx + 0.3 * v)
        vn = keep * v + coef[4, :, rows, :] + push * (fy - 0.3 * u)
        if not emit:
            uv[0, :, rows, :] = un
            uv[1, :, rows, :] = vn
            return
        mask = coef[5, :, rows, :]
        fx, fy = mask * fx, mask * fy
        out_rows = pl.ds(pl.multiple_of(base - TOP, 8), 8)
        for j in range(cols):
            at = pl.ds(j * LANES, LANES)
            o_vel[0, out_rows, at] = un[j]
            o_vel[1, out_rows, at] = vn[j]
            o_frc[0, out_rows, at] = fx[j]
            o_frc[1, out_rows, at] = fy[j]

    loop(0, tiles, stress_first)

    def subcycle(i, carry):
        loop(0, tiles, functools.partial(momentum, emit=False))
        loop(0, tiles, stress_next)
        return carry

    lax.fori_loop(0, NSUB - 1, subcycle, 0)

    def back1(d, sender):
        return to(
            sig.at[:, pl.ds(0, cols), pl.ds(TOP + d * piece, piece), :], back.at[sender],
            r1_s.at[d], r1_r.at[sender], lon=d,
        )

    peers(lambda d: back1(d, me).start())
    self3 = pltpu.make_async_copy(
        sig.at[:, pl.ds(0, cols), pl.ds(TOP + me * piece, piece), :], back.at[me], one_sem.at[5]
    )
    self3.start()
    loop(1, tiles - 1, functools.partial(momentum, emit=True))

    inv_copy.wait()
    peers(lambda d: back1(d, d).wait_recv())
    self3.wait()

    def refill(d):
        for s in range(slots):
            block = inv_sm[0, d * slots + s]
            got = back[lax.div(block, cols), :, lax.rem(block, cols)]
            home[d, s, 0] = 0.5 * (got[0] + got[1])
            home[d, s, 1] = 0.5 * (got[0] - got[1])
            home[d, s, 2] = 0.5 * got[2]

    def back2(d, sender):
        return to(
            home.at[d], o_sig.at[0, :, :, pl.ds(sender * piece, piece), :],
            r2_s.at[d], r2_r.at[sender], lon=d,
        )

    def send_back2(d):
        refill(d)
        back2(d, me).start()

    peers(send_back2)
    refill(me)
    self4 = pltpu.make_async_copy(
        home.at[me], o_sig.at[0, :, :, pl.ds(me * piece, piece), :], one_sem.at[6]
    )
    self4.start()
    self4.wait()
    peers(lambda d: back2(d, d).wait_recv())

    for c in x_copies + y_copies:
        c.wait_send()

    def drain(d):
        for make in (planmsg, stage1, stage2, back1, back2):
            make(d, me).wait_send()

    peers(drain)


def solution(mesh):
    n_lon, n_lat = mesh.shape["lon"], mesh.shape["lat"]

    def body(velocity_start, forcing, strength, mobility, plan, stress_in):
        cols, slots, side = plan.shape[1], stress_in.shape[1], stress_in.shape[-1]
        piece, wide, tall = side // n_lon, cols + 1, side + 32
        f32, i32 = jnp.float32, jnp.int32
        vmem, dma = pltpu.VMEM, pltpu.SemaphoreType.DMA
        anywhere = pl.BlockSpec(memory_space=pl.ANY)
        inside = pl.BlockSpec(memory_space=pltpu.VMEM)
        return tuple(pl.pallas_call(
            functools.partial(kernel, n_lon, n_lat),
            out_shape=(
                jax.ShapeDtypeStruct(velocity_start.shape, f32),
                jax.ShapeDtypeStruct(forcing.shape, f32),
                jax.ShapeDtypeStruct(stress_in.shape, f32),
            ),
            in_specs=[pl.BlockSpec(memory_space=pltpu.SMEM)] + [anywhere] * 5,
            out_specs=(inside, inside, inside),
            scratch_shapes=[
                vmem((7, wide, tall, LANES), f32),
                vmem((side, LANES), f32),
                vmem((side, LANES), f32),
                vmem((side, LANES), f32),
                vmem((side, LANES), f32),
                vmem((1, LANES), i32),
                vmem((n_lon, 1, LANES), i32),
                pltpu.SMEM((n_lon, 1, LANES), i32),
                vmem((1, LANES), i32),
                pltpu.SMEM((1, LANES), i32),
                vmem((n_lon * slots, 3, piece, LANES), f32),
                vmem((n_lon, 3, wide, piece, LANES), f32),
                vmem((3, wide, tall, LANES), f32),
                vmem((2, wide, tall, LANES), f32),
                vmem((6, wide, tall, LANES), f32),
                vmem((3, wide, tall, LANES), f32),
                vmem((n_lon, 3, cols, piece, LANES), f32),
                vmem((n_lon, slots, 3, piece, LANES), f32),
                dma((4 * cols,)),
                dma((7,)),
                dma((n_lon,)), dma((n_lon,)),
                dma((n_lon,)), dma((n_lon,)),
                dma((2,)), dma((2,)),
                dma((2,)), dma((2,)),
                dma((n_lon,)), dma((n_lon,)),
                dma((2,)), dma((2,)),
                dma((n_lon,)), dma((n_lon,)),
                dma((n_lon,)), dma((n_lon,)),
            ],
            compiler_params=pltpu.CompilerParams(collective_id=0, has_side_effects=True),
        )(plan, velocity_start, forcing, strength, mobility, stress_in))

    placed = (
        P(None, "lat", "lon"),
        P(None, "lat", "lon"),
        P("lat", "lon"),
        P("lat", "lon"),
        P("lat", "lon"),
        P("lat", "lon", None, None, None),
    )
    return jax.shard_map(
        body,
        mesh=mesh,
        in_specs=placed,
        out_specs=(P(None, "lat", "lon"), P(None, "lat", "lon"), P("lat", "lon", None, None, None)),
        check_vma=False,
    )
```

time: 684 us -> 73.5 us (0.11)
  the two profiles are of different devices: /device:TPU:96 before, /device:TPU:0 now
where the time goes in v1:
time: 73.5 us; the launch traced here: 73.4 us
  Pallas kernels  68.8 us (94%)
  local copies, waits for them, and re-layouts  3.86 us (5%)
    pallas_call x1, Pallas kernels, body(): pl.pallas_call(functools.partial(kernel, n_lon, n_lat), out_shape=(jax.Sh...  68.8 us
    unnamed x7, local copies, waits for them, and re-layouts  3.86 us

profile of v1, /device:TPU:0, one launch (start us, length us, event | category | flops | bytes accessed | tf_op | source)
XLA Modules:
  0.0 73.4 jit_solution(9891977084618726214)
XLA Ops:
  0.6 68.8 %shard_map.85 = (f32[2,128,512]{2,1,0:T(8,128)}, f32[2,128,512]{2,1,0:T(8,128)}, f32[1,2,3,128,128]{4,3,2,1,0:T(8,128)}) custom-call(s32[1,4]{1,0:T(1,128)} %plan_ref.1, f32[2,128,512]{2,1,0:T(8,128)} %vel_ref.1, f32[2,128,512]{2,1,0:T(8,128)} %frc_ref.1, f32[128,512]{1,0:T(8,128)} %str_ref.1, f32[128,512]{1,0:T(8,128)} %mob_ref.1, ...), custom_call_target="tpu_custom_call" | custom-call | tf_op jit(solution)/shard_map/pallas_call | solution.py:372
  69.5 0.0 copy-start
  69.5 1.9 %copy.12 = f32[2,128,512]{2,1,0:T(8,128)} copy(f32[2,128,512]{2,1,0:T(8,128)} %get-tuple-element.6) | data formatting | bytes 1048576
  71.4 0.0 copy-done
  71.4 0.0 copy-start.1
  71.4 0.8 %copy.13 = f32[2,128,512]{2,1,0:T(8,128)} copy(f32[2,128,512]{2,1,0:T(8,128)S(1)} %copy-done) | data formatting | bytes 1048576
  72.2 0.4 copy-done.1
  72.6 0.7 %copy.14 = f32[1,2,3,128,128]{4,3,2,1,0:T(8,128)} copy(f32[1,2,3,128,128]{4,3,2,1,0:T(8,128)S(1)} %copy-done.1) | data formatting | bytes 786432
Async XLA Ops:
  69.5 1.9 %copy-start = (f32[2,128,512]{2,1,0:T(8,128)S(1)}, f32[2,128,512]{2,1,0:T(8,128)}, u32[]{:S(2)}) copy-start(f32[2,128,512]{2,1,0:T(8,128)} %get-tuple-element.7) | copy-start | bytes 1572868
  71.4 1.2 %copy-start.1 = (f32[1,2,3,128,128]{4,3,2,1,0:T(8,128)S(1)}, f32[1,2,3,128,128]{4,3,2,1,0:T(8,128)}, u32[]{:S(2)}) copy-start(f32[1,2,3,128,128]{4,3,2,1,0:T(8,128)} %get-tuple-element.8) | copy-start | bytes 1179652

commit v2 on v1

v2 whole, which is shorter than its diff:
```python
import functools

import jax
import jax.numpy as jnp
from jax import lax
from jax.experimental import pallas as pl
from jax.experimental.pallas import tpu as pltpu
from jax.sharding import PartitionSpec as P

NSUB = 4
PARTS = 2
STRIDE = 7
UNROLL = 3
LANES = 128
HALO = 8
TOP = 16
MESH = pl.DeviceIdType.MESH


def kernel(
    n_lon, n_lat,
    plan_ref, vel_ref, frc_ref, str_ref, mob_ref, sig_ref,
    o_vel, o_frc, o_sig,
    cst, edge_l, edge_r, halo_r, halo_l,
    plan_own, plan_all, plan_sm, inv_own, inv_sm,
    part, pack, sig, uv, coef, inc, back, home,
    loc_sem, one_sem, self_sem, p1_s, p1_r, pl_s, pl_r, x_s, x_r, y_s, y_r,
    p2_s, p2_r, h_s, h_r, r1_s, r1_r, r2_s, r2_r,
):
    me = lax.axis_index("lon")
    lat = lax.axis_index("lat")
    right, left = lax.rem(me + 1, n_lon), lax.rem(me + n_lon - 1, n_lon)
    below, above = lax.rem(lat + 1, n_lat), lax.rem(lat + n_lat - 1, n_lat)
    side = LANES
    all_cols = plan_ref.shape[1]
    cols = all_cols // PARTS
    slots = sig_ref.shape[1]
    piece = side // n_lon
    tiles = (side + 2 * HALO) // 8
    lane1 = lax.broadcasted_iota(jnp.int32, (1, LANES), 1)
    lane = lax.broadcasted_iota(jnp.int32, (1, 1, LANES), 2)

    def to(src, dst, ss, rs, **where):
        return pltpu.make_async_remote_copy(
            src_ref=src, dst_ref=dst, send_sem=ss, recv_sem=rs,
            device_id=where, device_id_type=MESH,
        )

    def peers(fn):
        def step(k, carry):
            fn(lax.rem(me + k * STRIDE, n_lon))
            return carry
        lax.fori_loop(1, n_lon, step, 0)

    def rows_of(d):
        return pl.ds(TOP + d * piece, piece)

    barrier = pltpu.get_barrier_semaphore()
    peers(lambda d: pl.semaphore_signal(barrier, inc=1, device_id={"lon": d}, device_id_type=MESH))
    for other in (above, below):
        pl.semaphore_signal(barrier, inc=1, device_id={"lat": other}, device_id_type=MESH)

    own_rows = pl.ds(TOP, side)
    copies = []
    for j in range(all_cols):
        h, t = divmod(j, cols)
        src_cols = pl.ds(j * LANES, LANES)
        copies += [
            (vel_ref.at[:, :, src_cols], cst.at[h, pl.ds(0, 2), t, own_rows, :]),
            (frc_ref.at[:, :, src_cols], cst.at[h, pl.ds(2, 2), t, own_rows, :]),
            (str_ref.at[:, src_cols], cst.at[h, 4, t, own_rows, :]),
            (mob_ref.at[:, src_cols], cst.at[h, 5, t, own_rows, :]),
        ]
    copies = [pltpu.make_async_copy(s, d, loc_sem.at[i]) for i, (s, d) in enumerate(copies)]
    for c in copies:
        c.start()
    row = jnp.full((1, LANES), -1, jnp.int32)
    for j in range(all_cols):
        h, t = divmod(j, cols)
        row = jnp.where(lane1 == j, plan_ref[0, j], row)
        active = jnp.where(plan_ref[0, j] >= 0, 1.0, 0.0)
        cst[h, 6, t, own_rows, :] = jnp.full((side, LANES), active, jnp.float32)
    plan_own[...] = row
    for c in copies:
        c.wait()

    to_left = jnp.zeros((side, LANES), jnp.float32)
    to_right = jnp.zeros((side, LANES), jnp.float32)
    for f in range(7):
        first, last = cst[0, f, 0, own_rows, :], cst[PARTS - 1, f, cols - 1, own_rows, :]
        if f:
            first = pltpu.roll(first, HALO * f, 1)
            last = pltpu.roll(last, LANES - HALO * f, 1)
        to_left = jnp.where((lane1 >= HALO * f) & (lane1 < HALO * (f + 1)), first, to_left)
        to_right = jnp.where(
            (lane1 >= LANES - HALO * (f + 1)) & (lane1 < LANES - HALO * f), last, to_right
        )
    edge_l[...] = to_left
    edge_r[...] = to_right
    pl.semaphore_wait(barrier, n_lon + 1)

    def stage1(d, sender):
        return to(
            sig_ref.at[0, :, :, pl.ds(d * piece, piece), :],
            part.at[pl.ds(sender * slots, slots)],
            p1_s.at[d], p1_r.at[sender], lon=d,
        )

    def planmsg(d, sender):
        return to(plan_own, plan_all.at[sender], pl_s.at[d], pl_r.at[sender], lon=d)

    x_copies = [
        to(edge_l, halo_r, x_s.at[0], x_r.at[0], lon=left),
        to(edge_r, halo_l, x_s.at[1], x_r.at[1], lon=right),
    ]
    for c in x_copies:
        c.start()
    peers(lambda d: planmsg(d, me).start())
    peers(lambda d: stage1(d, me).start())
    self1 = pltpu.make_async_copy(
        sig_ref.at[0, :, :, pl.ds(me * piece, piece), :],
        part.at[pl.ds(me * slots, slots)], one_sem.at[0],
    )
    self1.start()
    self_plan = pltpu.make_async_copy(plan_own, plan_all.at[me], one_sem.at[1])
    self_plan.start()

    for c in x_copies:
        c.wait_recv()
    for f in range(7):
        from_r, from_l = halo_r[...], halo_l[...]
        if f:
            from_r = pltpu.roll(from_r, LANES - HALO * f, 1)
            from_l = pltpu.roll(from_l, HALO * f, 1)
        for h in range(PARTS):
            a = from_r if h == PARTS - 1 else cst[h + 1, f, 0, own_rows, :]
            b = from_l if h == 0 else cst[h - 1, f, cols - 1, own_rows, :]
            cst[h, f, cols, own_rows, :] = jnp.where(
                lane1 < HALO, a, jnp.where(lane1 >= LANES - HALO, b, 0.0)
            )
    y_copies = [
        to(cst.at[:, :, :, pl.ds(TOP, HALO), :], cst.at[:, :, :, pl.ds(TOP + side, HALO), :],
           y_s.at[0], y_r.at[0], lat=above),
        to(cst.at[:, :, :, pl.ds(TOP + side - HALO, HALO), :],
           cst.at[:, :, :, pl.ds(TOP - HALO, HALO), :],
           y_s.at[1], y_r.at[1], lat=below),
    ]
    for c in y_copies:
        c.start()

    peers(lambda d: planmsg(d, d).wait_recv())
    self_plan.wait()
    plan_copy = pltpu.make_async_copy(plan_all, plan_sm, one_sem.at[2])
    plan_copy.start()
    plan_copy.wait()

    peers(lambda d: stage1(d, d).wait_recv())
    self1.wait()

    def seat(d, j):
        return part[jnp.maximum(plan_sm[d, 0, j], 0)]

    def fill(h, d):
        for j in range(cols):
            block = seat(d, h * cols + j)
            for f in range(3):
                pack[h, d, f * cols + j] = block[f]
        if h == PARTS - 1:
            after = seat(lax.rem(d + 1, n_lon), 0)
        else:
            after = seat(d, (h + 1) * cols)
        if h == 0:
            before = seat(lax.rem(d + n_lon - 1, n_lon), all_cols - 1)
        else:
            before = seat(d, h * cols - 1)
        both = jnp.where(lane1 < LANES // 2, after[0], before[0])
        for f in range(1, 3):
            a = pltpu.roll(after[f], HALO * f, 1)
            b = pltpu.roll(before[f], LANES - HALO * f, 1)
            both = jnp.where((lane1 >= HALO * f) & (lane1 < HALO * (f + 1)), a, both)
            both = jnp.where((lane1 >= LANES - HALO * (f + 1)) & (lane1 < LANES - HALO * f), b, both)
        pack[h, d, 3 * cols] = both

    def stage2(h, d, sender):
        return to(
            pack.at[h, d], sig.at[h, :, rows_of(sender), :],
            p2_s.at[h * n_lon + d], p2_r.at[h * n_lon + sender], lon=d,
        )

    def self2(h):
        return pltpu.make_async_copy(pack.at[h, me], sig.at[h, :, rows_of(me), :], self_sem.at[h])

    for h in range(PARTS):
        def send2(d, h=h):
            fill(h, d)
            stage2(h, d, me).start()
        peers(send2)
        fill(h, me)
        self2(h).start()

    def invert(d, inv):
        for j in range(all_cols):
            inv = jnp.where(lane1 == plan_sm[d, 0, j], d * all_cols + j, inv)
        return inv
    inv_own[...] = lax.fori_loop(0, n_lon, invert, jnp.zeros((1, LANES), jnp.int32))
    inv_copy = pltpu.make_async_copy(inv_own, inv_sm, one_sem.at[3])
    inv_copy.start()

    def east(x):
        r = pltpu.roll(x, LANES - 1, 2)
        return jnp.where(lane == LANES - 1, jnp.concatenate([r[1:], r[:1]], 0), r)

    def west(x):
        r = pltpu.roll(x, 1, 2)
        return jnp.where(lane == 0, jnp.concatenate([r[-1:], r[:-1]], 0), r)

    def diff_x(x):
        return east(x) - west(x)

    def diff_y(ref, h, f, base):
        return ref[h, f, :, pl.ds(base + 1, 8), :] - ref[h, f, :, pl.ds(base - 1, 8), :]

    def increments(h, base, rows):
        u, v = uv[h, 0, :, rows, :], uv[h, 1, :, rows, :]
        ux, vx = diff_x(u), diff_x(v)
        uy, vy = diff_y(uv, h, 0, base), diff_y(uv, h, 1, base)
        div, ten, shr = ux + vy, ux - vy, uy + vx
        a = coef[h, 0, :, rows, :]
        ar = a * lax.rsqrt(div * div + 0.25 * (ten * ten + shr * shr) + 0.25)
        ten4 = 0.25 * ten
        return ar * (div + ten4) - a, ar * (div - ten4) - a, ar * (0.25 * shr)

    def tile(t):
        base = pl.multiple_of(HALO + 8 * t, 8)
        return base, pl.ds(base, 8)

    def loop(lo, hi, fn, unroll=1):
        def step(t, carry):
            fn(*tile(t))
            return carry
        lax.fori_loop(lo, hi, step, 0, unroll=unroll)

    for c in y_copies:
        c.wait_recv()

    def prepare(h, t):
        base, rows = tile(t)
        outside = ((t == 0) & (lat == 0)) | ((t == tiles - 1) & (lat == n_lat - 1))
        mask = cst[h, 6, :, rows, :] * jnp.where(outside, 0.0, 1.0)
        mob = cst[h, 5, :, rows, :]
        ratio = mask / (5.0 + mob)
        push = ratio * mob
        sx, sy = cst[h, 0, :, rows, :], cst[h, 1, :, rows, :]
        uv[h, 0, :, rows, :] = mask * sx
        uv[h, 1, :, rows, :] = mask * sy
        coef[h, 0, :, rows, :] = 0.2 * mask * cst[h, 4, :, rows, :]
        coef[h, 1, :, rows, :] = 4.0 * ratio
        coef[h, 2, :, rows, :] = push
        coef[h, 3, :, rows, :] = ratio * sx + push * cst[h, 2, :, rows, :]
        coef[h, 4, :, rows, :] = ratio * sy + push * cst[h, 3, :, rows, :]
        coef[h, 5, :, rows, :] = mask

    def warm_up(h, carry):
        def step(t, inner):
            prepare(h, t)
            return inner
        lax.fori_loop(0, tiles, step, 0)

        def first(base, rows):
            for f, value in enumerate(increments(h, base, rows)):
                inc[h, f, :, rows, :] = value
        loop(0, tiles, first)
        return carry

    lax.fori_loop(0, PARTS, warm_up, 0)

    def stress_first(h, base, rows):
        w = 0.8 * coef[h, 5, :, rows, :]
        beside = sig[h, 3 * cols, rows, :]
        s = []
        for f in range(3):
            extra = beside
            if f:
                extra = jnp.where(
                    lane1 < LANES // 2,
                    pltpu.roll(beside, LANES - HALO * f, 1), pltpu.roll(beside, HALO * f, 1),
                )
            s.append(jnp.concatenate([sig[h, pl.ds(f * cols, cols), rows, :], extra[None]], 0))
        inc[h, 0, :, rows, :] += w * (s[0] + s[1])
        inc[h, 1, :, rows, :] += w * (s[0] - s[1])
        inc[h, 2, :, rows, :] += (w + w) * s[2]

    def stress_next(h, base, rows):
        for f, value in enumerate(increments(h, base, rows)):
            inc[h, f, :, rows, :] = 0.8 * inc[h, f, :, rows, :] + value

    def momentum(h, base, rows, emit=False):
        fx = 0.25 * (diff_x(inc[h, 0, :, rows, :]) + diff_y(inc, h, 2, base))
        fy = 0.25 * (diff_x(inc[h, 2, :, rows, :]) + diff_y(inc, h, 1, base))
        u, v = uv[h, 0, :, rows, :], uv[h, 1, :, rows, :]
        keep, push = coef[h, 1, :, rows, :], coef[h, 2, :, rows, :]
        un = keep * u + coef[h, 3, :, rows, :] + push * (fx + 0.3 * v)
        vn = keep * v + coef[h, 4, :, rows, :] + push * (fy - 0.3 * u)
        if not emit:
            uv[h, 0, :, rows, :] = un
            uv[h, 1, :, rows, :] = vn
            return
        mask = coef[h, 5, :, rows, :]
        fx, fy = mask * fx, mask * fy
        out_rows = pl.ds(pl.multiple_of(base - TOP, 8), 8)
        for j in range(cols):
            at = pl.ds(pl.multiple_of((h * cols + j) * LANES, LANES), LANES)
            o_vel[0, out_rows, at] = un[j]
            o_vel[1, out_rows, at] = vn[j]
            o_frc[0, out_rows, at] = fx[j]
            o_frc[1, out_rows, at] = fy[j]

    def take(h, sender):
        @pl.when(sender != me)
        def _():
            stage2(h, sender, sender).wait_recv()

        @pl.when(sender == me)
        def _():
            self2(h).wait()

    def piece_tiles(d, fn):
        for i in range(piece // 8):
            base = pl.multiple_of(TOP + d * piece + 8 * i, 8)
            fn(base, pl.ds(base, 8))

    def back1(h, d, sender):
        return to(
            inc.at[h, :, pl.ds(0, cols), rows_of(d), :], back.at[sender, h],
            r1_s.at[h * n_lon + d], r1_r.at[h * n_lon + sender], lon=d,
        )

    def self3(h):
        return pltpu.make_async_copy(
            inc.at[h, :, pl.ds(0, cols), rows_of(me), :], back.at[me, h], self_sem.at[PARTS + h]
        )

    def run(h, carry):
        up = to(sig.at[h, :, pl.ds(TOP, HALO), :], sig.at[h, :, pl.ds(TOP + side, HALO), :],
                h_s.at[2 * h], h_r.at[2 * h], lat=above)
        down = to(sig.at[h, :, pl.ds(TOP + side - HALO, HALO), :],
                  sig.at[h, :, pl.ds(TOP - HALO, HALO), :],
                  h_s.at[2 * h + 1], h_r.at[2 * h + 1], lat=below)
        take(h, 0)
        up.start()
        take(h, n_lon - 1)
        down.start()
        first = functools.partial(stress_first, h)
        move = functools.partial(momentum, h)
        following = functools.partial(stress_next, h)

        def arrive(k, inner):
            sender = lax.rem(me + k * (n_lon - STRIDE % n_lon), n_lon)

            @pl.when((sender != 0) & (sender != n_lon - 1))
            def _():
                take(h, sender)
            piece_tiles(sender, first)
            return inner

        lax.fori_loop(0, n_lon, arrive, 0)
        loop(2, tiles - 2, move, 2)
        up.wait()
        down.wait()
        first(*tile(0))
        first(*tile(tiles - 1))
        for t in (0, 1, tiles - 2, tiles - 1):
            move(*tile(t))

        def subcycle(i, inner):
            loop(0, tiles, following, UNROLL)
            loop(0, tiles, move, UNROLL)
            return inner

        lax.fori_loop(0, NSUB - 2, subcycle, 0)

        def send_back1(d):
            piece_tiles(d, following)
            back1(h, d, me).start()

        peers(send_back1)
        piece_tiles(me, following)
        self3(h).start()
        following(*tile(0))
        following(*tile(tiles - 1))
        return carry

    lax.fori_loop(0, PARTS, run, 0)

    def finish(h, carry):
        loop(1, tiles - 1, functools.partial(momentum, h, emit=True), 2)
        return carry

    lax.fori_loop(0, PARTS, finish, 0)

    inv_copy.wait()
    for h in range(PARTS):
        peers(lambda d, h=h: back1(h, d, d).wait_recv())
        self3(h).wait()

    def refill(d):
        for s in range(slots):
            block = inv_sm[0, d * slots + s]
            owner, column = lax.div(block, all_cols), lax.rem(block, all_cols)
            got = back[owner, lax.div(column, cols), :, lax.rem(column, cols)]
            home[d, s, 0] = 0.5 * (got[0] + got[1])
            home[d, s, 1] = 0.5 * (got[0] - got[1])
            home[d, s, 2] = 0.5 * got[2]

    def back2(d, sender):
        return to(
            home.at[d], o_sig.at[0, :, :, pl.ds(sender * piece, piece), :],
            r2_s.at[d], r2_r.at[sender], lon=d,
        )

    def send_back2(d):
        refill(d)
        back2(d, me).start()

    peers(send_back2)
    refill(me)
    self4 = pltpu.make_async_copy(
        home.at[me], o_sig.at[0, :, :, pl.ds(me * piece, piece), :], one_sem.at[4]
    )
    self4.start()

    for c in x_copies + y_copies:
        c.wait_send()

    def drain(d):
        planmsg(d, me).wait_send()
        stage1(d, me).wait_send()
        for h in range(PARTS):
            stage2(h, d, me).wait_send()
            back1(h, d, me).wait_send()
        back2(d, me).wait_send()

    peers(drain)
    self4.wait()
    peers(lambda d: back2(d, d).wait_recv())


def hand_over(*refs):
    sources, targets, sem = refs[:3], refs[3:6], refs[6]
    moves = [pltpu.make_async_copy(s, t, sem.at[i]) for i, (s, t) in enumerate(zip(sources, targets))]
    for m in moves:
        m.start()
    for m in moves:
        m.wait()


def solution(mesh):
    n_lon, n_lat = mesh.shape["lon"], mesh.shape["lat"]

    def body(velocity_start, forcing, strength, mobility, plan, stress_in):
        cols, slots, side = plan.shape[1], stress_in.shape[1], stress_in.shape[-1]
        cols = cols // PARTS
        piece, wide, tall = side // n_lon, cols + 1, side + 32
        f32, i32 = jnp.float32, jnp.int32
        vmem, dma = pltpu.VMEM, pltpu.SemaphoreType.DMA
        anywhere = pl.BlockSpec(memory_space=pl.ANY)
        inside = pl.BlockSpec(memory_space=pltpu.VMEM)
        shapes = (velocity_start.shape, forcing.shape, stress_in.shape)
        results = pl.pallas_call(
            functools.partial(kernel, n_lon, n_lat),
            out_shape=tuple(vmem(s, f32) for s in shapes),
            in_specs=[pl.BlockSpec(memory_space=pltpu.SMEM)] + [anywhere] * 5,
            out_specs=(inside,) * 3,
            scratch_shapes=[
                vmem((PARTS, 7, wide, tall, LANES), f32),
                vmem((side, LANES), f32),
                vmem((side, LANES), f32),
                vmem((side, LANES), f32),
                vmem((side, LANES), f32),
                vmem((1, LANES), i32),
                vmem((n_lon, 1, LANES), i32),
                pltpu.SMEM((n_lon, 1, LANES), i32),
                vmem((1, LANES), i32),
                pltpu.SMEM((1, LANES), i32),
                vmem((n_lon * slots, 3, piece, LANES), f32),
                vmem((PARTS, n_lon, 3 * cols + 1, piece, LANES), f32),
                vmem((PARTS, 3 * cols + 1, tall, LANES), f32),
                vmem((PARTS, 2, wide, tall, LANES), f32),
                vmem((PARTS, 6, wide, tall, LANES), f32),
                vmem((PARTS, 3, wide, tall, LANES), f32),
                vmem((n_lon, PARTS, 3, cols, piece, LANES), f32),
                vmem((n_lon, slots, 3, piece, LANES), f32),
                dma((4 * cols * PARTS,)),
                dma((5,)),
                dma((2 * PARTS,)),
                dma((n_lon,)), dma((n_lon,)),
                dma((n_lon,)), dma((n_lon,)),
                dma((2,)), dma((2,)),
                dma((2,)), dma((2,)),
                dma((PARTS * n_lon,)), dma((PARTS * n_lon,)),
                dma((2 * PARTS,)), dma((2 * PARTS,)),
                dma((PARTS * n_lon,)), dma((PARTS * n_lon,)),
                dma((n_lon,)), dma((n_lon,)),
            ],
            compiler_params=pltpu.CompilerParams(collective_id=0, has_side_effects=True),
        )(plan, velocity_start, forcing, strength, mobility, stress_in)
        return tuple(pl.pallas_call(
            hand_over,
            out_shape=tuple(jax.ShapeDtypeStruct(s, f32) for s in shapes),
            in_specs=[inside] * 3,
            out_specs=(pl.BlockSpec(memory_space=pltpu.HBM),) * 3,
            scratch_shapes=[dma((3,))],
            compiler_params=pltpu.CompilerParams(vmem_limit_bytes=1 << 20),
        )(*results))

    placed = (
        P(None, "lat", "lon"),
        P(None, "lat", "lon"),
        P("lat", "lon"),
        P("lat", "lon"),
        P("lat", "lon"),
        P("lat", "lon", None, None, None),
    )
    return jax.shard_map(
        body,
        mesh=mesh,
        in_specs=placed,
        out_specs=(P(None, "lat", "lon"), P(None, "lat", "lon"), P("lat", "lon", None, None, None)),
        check_vma=False,
    )
```

time: 73.5 us -> 57.5 us (0.78); the launches traced: 73.4 us -> 56.6 us
  Pallas kernels: 68.8 us -> 55.9 us
  local copies, waits for them, and re-layouts: 3.86 us -> 0 us
    pallas_call x1 -> x2, Pallas kernels: 68.8 us -> 55.9 us  [the longest x1 54.8 us: body(): pl.pallas_call(functools.partial(kernel, n_lon, n_lat), out_shape=tuple((...]
    unnamed x7 -> x0, local copies, waits for them, and re-layouts: 3.86 us -> none
where the time goes in v2:
time: 57.5 us; the launch traced here: 56.6 us
  Pallas kernels  55.9 us (97%)
  between operations  0.64 us (1%)
    pallas_call x1, Pallas kernels, body(): pl.pallas_call(functools.partial(kernel, n_lon, n_lat), out_shape=tuple((...  54.8 us

profile of v2, /device:TPU:0, one launch (start us, length us, event | category | flops | bytes accessed | tf_op | source)
XLA Modules:
  0.0 56.6 jit_solution(18414174370363167924)
XLA Ops:
  0.6 54.8 %shard_map.85 = (f32[2,128,512]{2,1,0:T(8,128)S(1)}, f32[2,128,512]{2,1,0:T(8,128)S(1)}, f32[1,2,3,128,128]{4,3,2,1,0:T(8,128)S(1)}) custom-call(s32[1,4]{1,0:T(1,128)} %plan_ref.1, f32[2,128,512]{2,1,0:T(8,128)} %vel_ref.1, f32[2,128,512]{2,1,0:T(8,128)} %frc_ref.1, f32[128,512]{1,0:T(8,128)} %str_ref.1, f32[128,512]{1,0:T(8,128)} %mob_ref.1, ...), custom_call_target="tpu_custom_call" | custom-call | tf_op jit(solution)/shard_map/pallas_call | solution.py:469
  55.5 1.1 %shard_map.86 = (f32[2,128,512]{2,1,0:T(8,128)}, f32[2,128,512]{2,1,0:T(8,128)}, f32[1,2,3,128,128]{4,3,2,1,0:T(8,128)}) custom-call(f32[2,128,512]{2,1,0:T(8,128)S(1)} %get-tuple-element.6.refs_0_, f32[2,128,512]{2,1,0:T(8,128)S(1)} %get-tuple-element.7.refs_1_, f32[1,2,3,128,128]{4,3,2,1,0:T(8,128)S(1)} %get-tuple-element.8.refs_2_), custom_call_target="tpu_custom_call" | custom-call | tf_op jit(solution)/shard_map/pallas_call | solution.py:507

commit v3 on v2

--- a/solution.py
+++ b/solution.py
@@ -9,8 +9,9 @@
 
 NSUB = 4
 PARTS = 2
-STRIDE = 7
-UNROLL = 3
+STRIDE = 3
+DEPTH = 5
+DECAY = 0.8
 LANES = 128
 HALO = 8
 TOP = 16
@@ -220,12 +221,12 @@
     def diff_y(ref, h, f, base):
         return ref[h, f, :, pl.ds(base + 1, 8), :] - ref[h, f, :, pl.ds(base - 1, 8), :]
 
-    def increments(h, base, rows):
+    def increments(h, k, base, rows):
         u, v = uv[h, 0, :, rows, :], uv[h, 1, :, rows, :]
         ux, vx = diff_x(u), diff_x(v)
         uy, vy = diff_y(uv, h, 0, base), diff_y(uv, h, 1, base)
         div, ten, shr = ux + vy, ux - vy, uy + vx
-        a = coef[h, 0, :, rows, :]
+        a = DECAY ** -k * coef[h, 0, :, rows, :]
         ar = a * lax.rsqrt(div * div + 0.25 * (ten * ten + shr * shr) + 0.25)
         ten4 = 0.25 * ten
         return ar * (div + ten4) - a, ar * (div - ten4) - a, ar * (0.25 * shr)
@@ -267,15 +268,15 @@
         lax.fori_loop(0, tiles, step, 0)
 
         def first(base, rows):
-            for f, value in enumerate(increments(h, base, rows)):
+            for f, value in enumerate(increments(h, 1, base, rows)):
                 inc[h, f, :, rows, :] = value
-        loop(0, tiles, first)
+        loop(0, tiles, first, 6)
         return carry
 
     lax.fori_loop(0, PARTS, warm_up, 0)
 
     def stress_first(h, base, rows):
-        w = 0.8 * coef[h, 5, :, rows, :]
+        w = coef[h, 5, :, rows, :]
         beside = sig[h, 3 * cols, rows, :]
         s = []
         for f in range(3):
@@ -290,22 +291,24 @@
         inc[h, 1, :, rows, :] += w * (s[0] - s[1])
         inc[h, 2, :, rows, :] += (w + w) * s[2]
 
-    def stress_next(h, base, rows):
-        for f, value in enumerate(increments(h, base, rows)):
-            inc[h, f, :, rows, :] = 0.8 * inc[h, f, :, rows, :] + value
-
-    def momentum(h, base, rows, emit=False):
-        fx = 0.25 * (diff_x(inc[h, 0, :, rows, :]) + diff_y(inc, h, 2, base))
-        fy = 0.25 * (diff_x(inc[h, 2, :, rows, :]) + diff_y(inc, h, 1, base))
+    def stress_next(h, k, base, rows):
+        for f, value in enumerate(increments(h, k, base, rows)):
+            inc[h, f, :, rows, :] += value
+
+    def momentum(h, k, base, rows, emit=False):
+        scale = 0.25 * DECAY ** k
+        fx = diff_x(inc[h, 0, :, rows, :]) + diff_y(inc, h, 2, base)
+        fy = diff_x(inc[h, 2, :, rows, :]) + diff_y(inc, h, 1, base)
         u, v = uv[h, 0, :, rows, :], uv[h, 1, :, rows, :]
-        keep, push = coef[h, 1, :, rows, :], coef[h, 2, :, rows, :]
-        un = keep * u + coef[h, 3, :, rows, :] + push * (fx + 0.3 * v)
-        vn = keep * v + coef[h, 4, :, rows, :] + push * (fy - 0.3 * u)
+        keep, push = coef[h, 1, :, rows, :], scale * coef[h, 2, :, rows, :]
+        turn = 0.3 / scale
+        un = keep * u + coef[h, 3, :, rows, :] + push * (fx + turn * v)
+        vn = keep * v + coef[h, 4, :, rows, :] + push * (fy - turn * u)
         if not emit:
             uv[h, 0, :, rows, :] = un
             uv[h, 1, :, rows, :] = vn
             return
-        mask = coef[h, 5, :, rows, :]
+        mask = scale * coef[h, 5, :, rows, :]
         fx, fy = mask * fx, mask * fy
         out_rows = pl.ds(pl.multiple_of(base - TOP, 8), 8)
         for j in range(cols):
@@ -351,8 +354,9 @@
         take(h, n_lon - 1)
         down.start()
         first = functools.partial(stress_first, h)
-        move = functools.partial(momentum, h)
-        following = functools.partial(stress_next, h)
+        stages = []
+        for k in range(1, NSUB):
+            stages += [functools.partial(momentum, h, k), functools.partial(stress_next, h, k + 1)]
 
         def arrive(k, inner):
             sender = lax.rem(me + k * (n_lon - STRIDE % n_lon), n_lon)
@@ -364,36 +368,26 @@
             return inner
 
         lax.fori_loop(0, n_lon, arrive, 0)
-        loop(2, tiles - 2, move, 2)
+        for i in range(DEPTH):
+            loop(2 + i, tiles - 2 - i, stages[i], tiles - 4 - 2 * i)
         up.wait()
         down.wait()
         first(*tile(0))
         first(*tile(tiles - 1))
-        for t in (0, 1, tiles - 2, tiles - 1):
-            move(*tile(t))
-
-        def subcycle(i, inner):
-            loop(0, tiles, following, UNROLL)
-            loop(0, tiles, move, UNROLL)
-            return inner
-
-        lax.fori_loop(0, NSUB - 2, subcycle, 0)
-
-        def send_back1(d):
-            piece_tiles(d, following)
-            back1(h, d, me).start()
-
-        peers(send_back1)
-        piece_tiles(me, following)
+        for i, stage in enumerate(stages):
+            if i < DEPTH:
+                loop(0, 2 + i, stage, 2 + i)
+                loop(tiles - 2 - i, tiles, stage, 2 + i)
+            else:
+                loop(0, tiles, stage, tiles)
+        peers(lambda d: back1(h, d, me).start())
         self3(h).start()
-        following(*tile(0))
-        following(*tile(tiles - 1))
         return carry
 
     lax.fori_loop(0, PARTS, run, 0)
 
     def finish(h, carry):
-        loop(1, tiles - 1, functools.partial(momentum, h, emit=True), 2)
+        loop(1, tiles - 1, functools.partial(momentum, h, NSUB, emit=True), 8)
         return carry
 
     lax.fori_loop(0, PARTS, finish, 0)
@@ -408,9 +402,10 @@
             block = inv_sm[0, d * slots + s]
             owner, column = lax.div(block, all_cols), lax.rem(block, all_cols)
             got = back[owner, lax.div(column, cols), :, lax.rem(column, cols)]
-            home[d, s, 0] = 0.5 * (got[0] + got[1])
-            home[d, s, 1] = 0.5 * (got[0] - got[1])
-            home[d, s, 2] = 0.5 * got[2]
+            got = (0.5 * DECAY ** NSUB) * got
+            home[d, s, 0] = got[0] + got[1]
+            home[d, s, 1] = got[0] - got[1]
+            home[d, s, 2] = got[2]
 
     def back2(d, sender):
         return to(

time: 57.5 us -> 50.4 us (0.88); the launches traced: 56.6 us -> 50.2 us
  Pallas kernels: 55.9 us -> 49.6 us
    pallas_call x1, Pallas kernels: 54.8 us -> 48.5 us  [body(): pl.pallas_call(functools.partial(kernel, n_lon, n_lat), out_shape=tuple((...]
where the time goes in v3:
time: 50.4 us; the launch traced here: 50.2 us
  Pallas kernels  49.6 us (98%)
  between operations  0.64 us (1%)
    pallas_call x1, Pallas kernels, body(): pl.pallas_call(functools.partial(kernel, n_lon, n_lat), out_shape=tuple((...  48.5 us
    pallas_call x1, Pallas kernels, body(): pl.pallas_call(hand_over, out_shape=tuple((jax.ShapeDtypeStruct(s, f32) f...  1.12 us

profile of v3, /device:TPU:0, one launch (start us, length us, event | category | flops | bytes accessed | tf_op | source)
XLA Modules:
  0.0 50.2 jit_solution(10115615994226917166)
XLA Ops:
  0.6 48.5 %shard_map.85 = (f32[2,128,512]{2,1,0:T(8,128)S(1)}, f32[2,128,512]{2,1,0:T(8,128)S(1)}, f32[1,2,3,128,128]{4,3,2,1,0:T(8,128)S(1)}) custom-call(s32[1,4]{1,0:T(1,128)} %plan_ref.1, f32[2,128,512]{2,1,0:T(8,128)} %vel_ref.1, f32[2,128,512]{2,1,0:T(8,128)} %frc_ref.1, f32[128,512]{1,0:T(8,128)} %str_ref.1, f32[128,512]{1,0:T(8,128)} %mob_ref.1, ...), custom_call_target="tpu_custom_call" | custom-call | tf_op jit(solution)/shard_map/pallas_call | solution.py:464
  49.1 1.1 %shard_map.86 = (f32[2,128,512]{2,1,0:T(8,128)}, f32[2,128,512]{2,1,0:T(8,128)}, f32[1,2,3,128,128]{4,3,2,1,0:T(8,128)}) custom-call(f32[2,128,512]{2,1,0:T(8,128)S(1)} %get-tuple-element.6.refs_0_, f32[2,128,512]{2,1,0:T(8,128)S(1)} %get-tuple-element.7.refs_1_, f32[1,2,3,128,128]{4,3,2,1,0:T(8,128)S(1)} %get-tuple-element.8.refs_2_), custom_call_target="tpu_custom_call" | custom-call | tf_op jit(solution)/shard_map/pallas_call | solution.py:502

commit v4 on v3

--- a/solution.py
+++ b/solution.py
@@ -9,13 +9,14 @@
 
 NSUB = 4
 PARTS = 2
-STRIDE = 3
+FAR_FIRST = (10, 6, 14, 9, 11, 2, 8, 5, 15, 7, 13, 1, 4, 3, 12)
 DEPTH = 5
 DECAY = 0.8
 LANES = 128
 HALO = 8
 TOP = 16
 MESH = pl.DeviceIdType.MESH
+SPLIT = (pl.ds(2, 1), pl.ds(0, 2))
 
 
 def kernel(
@@ -24,8 +25,8 @@
     o_vel, o_frc, o_sig,
     cst, edge_l, edge_r, halo_r, halo_l,
     plan_own, plan_all, plan_sm, inv_own, inv_sm,
-    part, pack, sig, uv, coef, inc, back, home,
-    loc_sem, one_sem, self_sem, p1_s, p1_r, pl_s, pl_r, x_s, x_r, y_s, y_r,
+    part_a, part_b, pack, sig, uv, coef, inc, back_a, back_b, home,
+    loc_sem, one_sem, first_sem, self_sem, p1_s, p1_r, pl_s, pl_r, x_s, x_r, y_s, y_r,
     p2_s, p2_r, h_s, h_r, r1_s, r1_r, r2_s, r2_r,
 ):
     me = lax.axis_index("lon")
@@ -47,17 +48,29 @@
             device_id=where, device_id_type=MESH,
         )
 
-    def peers(fn):
+    def each(fn):
         def step(k, carry):
-            fn(lax.rem(me + k * STRIDE, n_lon))
+            fn(lax.rem(me + k, n_lon))
             return carry
         lax.fori_loop(1, n_lon, step, 0)
 
+    if n_lon == 16:
+        y, x = lax.div(me, 4), lax.rem(me, 4)
+        ahead = [4 * lax.rem(y + i // 4, 4) + lax.rem(x + i % 4, 4) for i in FAR_FIRST]
+        behind = [4 * lax.rem(y + 4 - i // 4, 4) + lax.rem(x + 4 - i % 4, 4) for i in FAR_FIRST]
+    else:
+        ahead = [lax.rem(me + i, n_lon) for i in range(1, n_lon)]
+        behind = [lax.rem(me + n_lon - i, n_lon) for i in range(1, n_lon)]
+
+    def peers(fn, sign=1):
+        for d in ahead if sign > 0 else behind:
+            fn(d)
+
     def rows_of(d):
         return pl.ds(TOP + d * piece, piece)
 
     barrier = pltpu.get_barrier_semaphore()
-    peers(lambda d: pl.semaphore_signal(barrier, inc=1, device_id={"lon": d}, device_id_type=MESH))
+    each(lambda d: pl.semaphore_signal(barrier, inc=1, device_id={"lon": d}, device_id_type=MESH))
     for other in (above, below):
         pl.semaphore_signal(barrier, inc=1, device_id={"lat": other}, device_id_type=MESH)
 
@@ -96,15 +109,20 @@
         to_right = jnp.where(
             (lane1 >= LANES - HALO * (f + 1)) & (lane1 < LANES - HALO * f), last, to_right
         )
-    edge_l[...] = to_left
-    edge_r[...] = to_right
+    half = side // 2
+    low = lane1 < LANES // 2
+    edge_l[...] = jnp.where(low, to_left[:half], pltpu.roll(to_left[half:], LANES // 2, 1))
+    edge_r[...] = jnp.where(low, pltpu.roll(to_right[half:], LANES // 2, 1), to_right[:half])
     pl.semaphore_wait(barrier, n_lon + 1)
 
-    def stage1(d, sender):
+    part, back = (part_a, part_b), (back_a, back_b)
+
+    def stage1(c, d, sender):
+        fields = SPLIT[c]
         return to(
-            sig_ref.at[0, :, :, pl.ds(d * piece, piece), :],
-            part.at[pl.ds(sender * slots, slots)],
-            p1_s.at[d], p1_r.at[sender], lon=d,
+            sig_ref.at[0, :, fields, pl.ds(d * piece, piece), :],
+            part[c].at[pl.ds(sender * slots, slots)],
+            p1_s.at[c * n_lon + d], p1_r.at[c * n_lon + sender], lon=d,
         )
 
     def planmsg(d, sender):
@@ -116,20 +134,27 @@
     ]
     for c in x_copies:
         c.start()
-    peers(lambda d: planmsg(d, me).start())
-    peers(lambda d: stage1(d, me).start())
-    self1 = pltpu.make_async_copy(
-        sig_ref.at[0, :, :, pl.ds(me * piece, piece), :],
-        part.at[pl.ds(me * slots, slots)], one_sem.at[0],
-    )
-    self1.start()
+    each(lambda d: planmsg(d, me).start())
+    for c in range(2):
+        peers(lambda d, c=c: stage1(c, d, me).start())
+    self1 = [
+        pltpu.make_async_copy(
+            sig_ref.at[0, :, SPLIT[c], pl.ds(me * piece, piece), :],
+            part[c].at[pl.ds(me * slots, slots)], first_sem.at[c],
+        )
+        for c in range(2)
+    ]
+    for c in self1:
+        c.start()
     self_plan = pltpu.make_async_copy(plan_own, plan_all.at[me], one_sem.at[1])
     self_plan.start()
 
     for c in x_copies:
         c.wait_recv()
     for f in range(7):
-        from_r, from_l = halo_r[...], halo_l[...]
+        from_r, from_l = (
+            jnp.concatenate([got[...], pltpu.roll(got[...], LANES // 2, 1)], 0) for got in (halo_r, halo_l)
+        )
         if f:
             from_r = pltpu.roll(from_r, LANES - HALO * f, 1)
             from_l = pltpu.roll(from_l, HALO * f, 1)
@@ -149,55 +174,70 @@
     for c in y_copies:
         c.start()
 
-    peers(lambda d: planmsg(d, d).wait_recv())
+    each(lambda d: planmsg(d, d).wait_recv())
     self_plan.wait()
     plan_copy = pltpu.make_async_copy(plan_all, plan_sm, one_sem.at[2])
     plan_copy.start()
     plan_copy.wait()
 
-    peers(lambda d: stage1(d, d).wait_recv())
-    self1.wait()
-
-    def seat(d, j):
-        return part[jnp.maximum(plan_sm[d, 0, j], 0)]
-
-    def fill(h, d):
+    for c in self1:
+        c.wait()
+
+    def seat(c, d, j):
+        return part[c][jnp.maximum(plan_sm[d, 0, j], 0)]
+
+    def fill_first(h, d):
         for j in range(cols):
-            block = seat(d, h * cols + j)
+            pack[h, d, j] = seat(0, d, h * cols + j)[0]
+
+    def fill_rest(h, d):
+        for j in range(cols):
+            block = seat(1, d, h * cols + j)
+            pack[h, d, cols + j] = block[0]
+            pack[h, d, 2 * cols + j] = block[1]
+        if h:
+            return
+        both = jnp.zeros((piece, LANES), jnp.float32)
+        for g in range(PARTS):
+            after = (d, (g + 1) * cols) if g < PARTS - 1 else (lax.rem(d + 1, n_lon), 0)
+            before = (d, g * cols - 1) if g else (lax.rem(d + n_lon - 1, n_lon), all_cols - 1)
             for f in range(3):
-                pack[h, d, f * cols + j] = block[f]
-        if h == PARTS - 1:
-            after = seat(lax.rem(d + 1, n_lon), 0)
-        else:
-            after = seat(d, (h + 1) * cols)
-        if h == 0:
-            before = seat(lax.rem(d + n_lon - 1, n_lon), all_cols - 1)
-        else:
-            before = seat(d, h * cols - 1)
-        both = jnp.where(lane1 < LANES // 2, after[0], before[0])
-        for f in range(1, 3):
-            a = pltpu.roll(after[f], HALO * f, 1)
-            b = pltpu.roll(before[f], LANES - HALO * f, 1)
-            both = jnp.where((lane1 >= HALO * f) & (lane1 < HALO * (f + 1)), a, both)
-            both = jnp.where((lane1 >= LANES - HALO * (f + 1)) & (lane1 < LANES - HALO * f), b, both)
-        pack[h, d, 3 * cols] = both
-
-    def stage2(h, d, sender):
+                i = 3 * g + f
+                c, at = (1, f) if f < 2 else (0, 0)
+                a, b = seat(c, *after)[at], seat(c, *before)[at]
+                if i:
+                    a, b = pltpu.roll(a, HALO * i, 1), pltpu.roll(b, LANES - HALO * i, 1)
+                both = jnp.where((lane1 >= HALO * i) & (lane1 < HALO * (i + 1)), a, both)
+                both = jnp.where((lane1 >= LANES - HALO * (i + 1)) & (lane1 < LANES - HALO * i), b, both)
+        pack[0, d, 3 * cols] = both
+
+    def width(h):
+        return 3 * cols + (1 if h == 0 else 0)
+
+    def stage2(h, c, d, sender):
+        span = pl.ds(0, cols) if c == 0 else pl.ds(cols, width(h) - cols)
+        slot = (2 * h + c) * n_lon
         return to(
-            pack.at[h, d], sig.at[h, :, rows_of(sender), :],
-            p2_s.at[h * n_lon + d], p2_r.at[h * n_lon + sender], lon=d,
+            pack.at[h, d, span], sig.at[h, span, rows_of(sender), :],
+            p2_s.at[slot + d], p2_r.at[slot + sender], lon=d,
         )
 
     def self2(h):
-        return pltpu.make_async_copy(pack.at[h, me], sig.at[h, :, rows_of(me), :], self_sem.at[h])
-
-    for h in range(PARTS):
-        def send2(d, h=h):
-            fill(h, d)
-            stage2(h, d, me).start()
-        peers(send2)
-        fill(h, me)
-        self2(h).start()
+        span = pl.ds(0, width(h))
+        return pltpu.make_async_copy(
+            pack.at[h, me, span], sig.at[h, span, rows_of(me), :], self_sem.at[h]
+        )
+
+    for c, fill in enumerate((fill_first, fill_rest)):
+        each(lambda d, c=c: stage1(c, d, d).wait_recv())
+        for h in range(PARTS):
+            def send2(d, h=h, c=c, fill=fill):
+                fill(h, d)
+                stage2(h, c, d, me).start()
+            peers(send2)
+            fill(h, me)
+            if c == 1:
+                self2(h).start()
 
     def invert(d, inv):
         for j in range(all_cols):
@@ -277,16 +317,17 @@
 
     def stress_first(h, base, rows):
         w = coef[h, 5, :, rows, :]
-        beside = sig[h, 3 * cols, rows, :]
+        beside = sig[0, 3 * cols, rows, :]
         s = []
         for f in range(3):
+            i, at = 3 * h + f, (1, 2, 0)[f] * cols
             extra = beside
-            if f:
+            if i:
                 extra = jnp.where(
                     lane1 < LANES // 2,
-                    pltpu.roll(beside, LANES - HALO * f, 1), pltpu.roll(beside, HALO * f, 1),
+                    pltpu.roll(beside, LANES - HALO * i, 1), pltpu.roll(beside, HALO * i, 1),
                 )
-            s.append(jnp.concatenate([sig[h, pl.ds(f * cols, cols), rows, :], extra[None]], 0))
+            s.append(jnp.concatenate([sig[h, pl.ds(at, cols), rows, :], extra[None]], 0))
         inc[h, 0, :, rows, :] += w * (s[0] + s[1])
         inc[h, 1, :, rows, :] += w * (s[0] - s[1])
         inc[h, 2, :, rows, :] += (w + w) * s[2]
@@ -321,7 +362,8 @@
     def take(h, sender):
         @pl.when(sender != me)
         def _():
-            stage2(h, sender, sender).wait_recv()
+            for c in range(2):
+                stage2(h, c, sender, sender).wait_recv()
 
         @pl.when(sender == me)
         def _():
@@ -332,22 +374,25 @@
             base = pl.multiple_of(TOP + d * piece + 8 * i, 8)
             fn(base, pl.ds(base, 8))
 
-    def back1(h, d, sender):
+    def back1(h, c, d, sender):
+        fields, slot = SPLIT[c], (2 * h + c) * n_lon
         return to(
-            inc.at[h, :, pl.ds(0, cols), rows_of(d), :], back.at[sender, h],
-            r1_s.at[h * n_lon + d], r1_r.at[h * n_lon + sender], lon=d,
-        )
-
-    def self3(h):
+            inc.at[h, fields, pl.ds(0, cols), rows_of(d), :], back[c].at[sender, h],
+            r1_s.at[slot + d], r1_r.at[slot + sender], lon=d,
+        )
+
+    def self3(h, c):
         return pltpu.make_async_copy(
-            inc.at[h, :, pl.ds(0, cols), rows_of(me), :], back.at[me, h], self_sem.at[PARTS + h]
-        )
-
-    def run(h, carry):
-        up = to(sig.at[h, :, pl.ds(TOP, HALO), :], sig.at[h, :, pl.ds(TOP + side, HALO), :],
+            inc.at[h, SPLIT[c], pl.ds(0, cols), rows_of(me), :], back[c].at[me, h],
+            self_sem.at[PARTS + 2 * h + c],
+        )
+
+    def run(h):
+        span = pl.ds(0, width(h))
+        up = to(sig.at[h, span, pl.ds(TOP, HALO), :], sig.at[h, span, pl.ds(TOP + side, HALO), :],
                 h_s.at[2 * h], h_r.at[2 * h], lat=above)
-        down = to(sig.at[h, :, pl.ds(TOP + side - HALO, HALO), :],
-                  sig.at[h, :, pl.ds(TOP - HALO, HALO), :],
+        down = to(sig.at[h, span, pl.ds(TOP + side - HALO, HALO), :],
+                  sig.at[h, span, pl.ds(TOP - HALO, HALO), :],
                   h_s.at[2 * h + 1], h_r.at[2 * h + 1], lat=below)
         take(h, 0)
         up.start()
@@ -358,16 +403,14 @@
         for k in range(1, NSUB):
             stages += [functools.partial(momentum, h, k), functools.partial(stress_next, h, k + 1)]
 
-        def arrive(k, inner):
-            sender = lax.rem(me + k * (n_lon - STRIDE % n_lon), n_lon)
-
+        def arrive(sender):
             @pl.when((sender != 0) & (sender != n_lon - 1))
             def _():
                 take(h, sender)
             piece_tiles(sender, first)
-            return inner
-
-        lax.fori_loop(0, n_lon, arrive, 0)
+
+        peers(arrive, -1)
+        arrive(me)
         for i in range(DEPTH):
             loop(2 + i, tiles - 2 - i, stages[i], tiles - 4 - 2 * i)
         up.wait()
@@ -380,11 +423,13 @@
                 loop(tiles - 2 - i, tiles, stage, 2 + i)
             else:
                 loop(0, tiles, stage, tiles)
-        peers(lambda d: back1(h, d, me).start())
-        self3(h).start()
-        return carry
-
-    lax.fori_loop(0, PARTS, run, 0)
+        for c in range(2):
+            peers(lambda d, c=c: back1(h, c, d, me).start())
+        for c in range(2):
+            self3(h, c).start()
+
+    for h in range(PARTS):
+        run(h)
 
     def finish(h, carry):
         loop(1, tiles - 1, functools.partial(momentum, h, NSUB, emit=True), 8)
@@ -392,33 +437,40 @@
 
     lax.fori_loop(0, PARTS, finish, 0)
 
-    inv_copy.wait()
-    for h in range(PARTS):
-        peers(lambda d, h=h: back1(h, d, d).wait_recv())
-        self3(h).wait()
-
-    def refill(d):
+    def refill(c, d):
         for s in range(slots):
             block = inv_sm[0, d * slots + s]
             owner, column = lax.div(block, all_cols), lax.rem(block, all_cols)
-            got = back[owner, lax.div(column, cols), :, lax.rem(column, cols)]
-            got = (0.5 * DECAY ** NSUB) * got
-            home[d, s, 0] = got[0] + got[1]
-            home[d, s, 1] = got[0] - got[1]
-            home[d, s, 2] = got[2]
-
-    def back2(d, sender):
+            h, j = lax.div(column, cols), lax.rem(column, cols)
+            scale = 0.5 * DECAY ** NSUB
+            if c == 0:
+                home[d, s, 2] = scale * back[0][owner, h, 0, j]
+            if c == 1:
+                plus, minus = scale * back[1][owner, h, 0, j], scale * back[1][owner, h, 1, j]
+                home[d, s, 0] = plus + minus
+                home[d, s, 1] = plus - minus
+
+    def back2(c, d, sender):
+        fields = SPLIT[c]
         return to(
-            home.at[d], o_sig.at[0, :, :, pl.ds(sender * piece, piece), :],
-            r2_s.at[d], r2_r.at[sender], lon=d,
-        )
-
-    def send_back2(d):
-        refill(d)
-        back2(d, me).start()
-
-    peers(send_back2)
-    refill(me)
+            home.at[d, :, fields], o_sig.at[0, :, fields, pl.ds(sender * piece, piece), :],
+            r2_s.at[c * n_lon + d], r2_r.at[c * n_lon + sender], lon=d,
+        )
+
+    inv_copy.wait()
+    for h in range(PARTS):
+        for c in range(2):
+            self3(h, c).wait()
+    for c in range(2):
+        for h in range(PARTS):
+            each(lambda d, h=h, c=c: back1(h, c, d, d).wait_recv())
+
+        def send_back2(d, c=c):
+            refill(c, d)
+            back2(c, d, me).start()
+
+        peers(send_back2)
+        refill(c, me)
     self4 = pltpu.make_async_copy(
         home.at[me], o_sig.at[0, :, :, pl.ds(me * piece, piece), :], one_sem.at[4]
     )
@@ -429,15 +481,19 @@
 
     def drain(d):
         planmsg(d, me).wait_send()
-        stage1(d, me).wait_send()
-        for h in range(PARTS):
-            stage2(h, d, me).wait_send()
-            back1(h, d, me).wait_send()
-        back2(d, me).wait_send()
-
-    peers(drain)
+        for c in range(2):
+            stage1(c, d, me).wait_send()
+            for h in range(PARTS):
+                stage2(h, c, d, me).wait_send()
+        for c in range(2):
+            for h in range(PARTS):
+                back1(h, c, d, me).wait_send()
+            back2(c, d, me).wait_send()
+
+    each(drain)
     self4.wait()
-    peers(lambda d: back2(d, d).wait_recv())
+    for c in range(2):
+        each(lambda d, c=c: back2(c, d, d).wait_recv())
 
 
 def hand_over(*refs):
@@ -468,34 +524,37 @@
             out_specs=(inside,) * 3,
             scratch_shapes=[
                 vmem((PARTS, 7, wide, tall, LANES), f32),
-                vmem((side, LANES), f32),
-                vmem((side, LANES), f32),
-                vmem((side, LANES), f32),
-                vmem((side, LANES), f32),
+                vmem((side // 2, LANES), f32),
+                vmem((side // 2, LANES), f32),
+                vmem((side // 2, LANES), f32),
+                vmem((side // 2, LANES), f32),
                 vmem((1, LANES), i32),
                 vmem((n_lon, 1, LANES), i32),
                 pltpu.SMEM((n_lon, 1, LANES), i32),
                 vmem((1, LANES), i32),
                 pltpu.SMEM((1, LANES), i32),
-                vmem((n_lon * slots, 3, piece, LANES), f32),
+                vmem((n_lon * slots, 1, piece, LANES), f32),
+                vmem((n_lon * slots, 2, piece, LANES), f32),
                 vmem((PARTS, n_lon, 3 * cols + 1, piece, LANES), f32),
                 vmem((PARTS, 3 * cols + 1, tall, LANES), f32),
                 vmem((PARTS, 2, wide, tall, LANES), f32),
                 vmem((PARTS, 6, wide, tall, LANES), f32),
                 vmem((PARTS, 3, wide, tall, LANES), f32),
-                vmem((n_lon, PARTS, 3, cols, piece, LANES), f32),
+                vmem((n_lon, PARTS, 1, cols, piece, LANES), f32),
+                vmem((n_lon, PARTS, 2, cols, piece, LANES), f32),
                 vmem((n_lon, slots, 3, piece, LANES), f32),
                 dma((4 * cols * PARTS,)),
                 dma((5,)),
-                dma((2 * PARTS,)),
-                dma((n_lon,)), dma((n_lon,)),
+                dma((2,)),
+                dma((3 * PARTS,)),
+                dma((2 * n_lon,)), dma((2 * n_lon,)),
                 dma((n_lon,)), dma((n_lon,)),
                 dma((2,)), dma((2,)),
                 dma((2,)), dma((2,)),
-                dma((PARTS * n_lon,)), dma((PARTS * n_lon,)),
+                dma((2 * PARTS * n_lon,)), dma((2 * PARTS * n_lon,)),
                 dma((2 * PARTS,)), dma((2 * PARTS,)),
-                dma((PARTS * n_lon,)), dma((PARTS * n_lon,)),
-                dma((n_lon,)), dma((n_lon,)),
+                dma((2 * PARTS * n_lon,)), dma((2 * PARTS * n_lon,)),
+                dma((2 * n_lon,)), dma((2 * n_lon,)),
             ],
             compiler_params=pltpu.CompilerParams(collective_id=0, has_side_effects=True),
         )(plan, velocity_start, forcing, strength, mobility, stress_in)

time: 50.4 us -> 49 us (0.972)
  Pallas kernels: 49.6 us -> 48.2 us
    pallas_call x1, Pallas kernels: 48.5 us -> 47.1 us  [body(): pl.pallas_call(functools.partial(kernel, n_lon, n_lat), out_shape=tuple((...]
where the time goes in v4:
time: 49 us; the launch traced here: 48.8 us
  Pallas kernels  48.2 us (98%)
  between operations  0.64 us (1%)
    pallas_call x1, Pallas kernels, body(): pl.pallas_call(functools.partial(kernel, n_lon, n_lat), out_shape=tuple((...  47.1 us
    pallas_call x1, Pallas kernels, body(): pl.pallas_call(hand_over, out_shape=tuple((jax.ShapeDtypeStruct(s, f32) f...  1.12 us

profile of v4, /device:TPU:0, one launch (start us, length us, event | category | flops | bytes accessed | tf_op | source)
XLA Modules:
  0.0 48.8 jit_solution(16423994819985332552)
XLA Ops:
  0.6 47.1 %shard_map.85 = (f32[2,128,512]{2,1,0:T(8,128)S(1)}, f32[2,128,512]{2,1,0:T(8,128)S(1)}, f32[1,2,3,128,128]{4,3,2,1,0:T(8,128)S(1)}) custom-call(s32[1,4]{1,0:T(1,128)} %plan_ref.1, f32[2,128,512]{2,1,0:T(8,128)} %vel_ref.1, f32[2,128,512]{2,1,0:T(8,128)} %frc_ref.1, f32[128,512]{1,0:T(8,128)} %str_ref.1, f32[128,512]{1,0:T(8,128)} %mob_ref.1, ...), custom_call_target="tpu_custom_call" | custom-call | tf_op jit(solution)/shard_map/pallas_call | solution.py:520
  47.7 1.1 %shard_map.86 = (f32[2,128,512]{2,1,0:T(8,128)}, f32[2,128,512]{2,1,0:T(8,128)}, f32[1,2,3,128,128]{4,3,2,1,0:T(8,128)}) custom-call(f32[2,128,512]{2,1,0:T(8,128)S(1)} %get-tuple-element.6.refs_0_, f32[2,128,512]{2,1,0:T(8,128)S(1)} %get-tuple-element.7.refs_1_, f32[1,2,3,128,128]{4,3,2,1,0:T(8,128)S(1)} %get-tuple-element.8.refs_2_), custom_call_target="tpu_custom_call" | custom-call | tf_op jit(solution)/shard_map/pallas_call | solution.py:561

commit v5 on v4

--- a/solution.py
+++ b/solution.py
@@ -9,7 +9,7 @@
 
 NSUB = 4
 PARTS = 2
-FAR_FIRST = (10, 6, 14, 9, 11, 2, 8, 5, 15, 7, 13, 1, 4, 3, 12)
+FAR_FIRST = (10, 9, 11, 6, 14, 5, 15, 7, 13, 2, 8, 1, 3, 4, 12)
 DEPTH = 5
 DECAY = 0.8
 LANES = 128
@@ -70,7 +70,7 @@
         return pl.ds(TOP + d * piece, piece)
 
     barrier = pltpu.get_barrier_semaphore()
-    each(lambda d: pl.semaphore_signal(barrier, inc=1, device_id={"lon": d}, device_id_type=MESH))
+    peers(lambda d: pl.semaphore_signal(barrier, inc=1, device_id={"lon": d}, device_id_type=MESH))
     for other in (above, below):
         pl.semaphore_signal(barrier, inc=1, device_id={"lat": other}, device_id_type=MESH)
 
@@ -217,6 +217,11 @@
     def stage2(h, c, d, sender):
         span = pl.ds(0, cols) if c == 0 else pl.ds(cols, width(h) - cols)
         slot = (2 * h + c) * n_lon
+        if c == 0:
+            return to(
+                pack.at[:, d, span], sig.at[:, span, rows_of(sender), :],
+                p2_s.at[d], p2_r.at[sender], lon=d,
+            )
         return to(
             pack.at[h, d, span], sig.at[h, span, rows_of(sender), :],
             p2_s.at[slot + d], p2_r.at[slot + sender], lon=d,
@@ -228,16 +233,23 @@
             pack.at[h, me, span], sig.at[h, span, rows_of(me), :], self_sem.at[h]
         )
 
-    for c, fill in enumerate((fill_first, fill_rest)):
-        each(lambda d, c=c: stage1(c, d, d).wait_recv())
+    def send_first(d):
         for h in range(PARTS):
-            def send2(d, h=h, c=c, fill=fill):
-                fill(h, d)
-                stage2(h, c, d, me).start()
-            peers(send2)
-            fill(h, me)
-            if c == 1:
-                self2(h).start()
+            fill_first(h, d)
+        stage2(0, 0, d, me).start()
+
+    each(lambda d: stage1(0, d, d).wait_recv())
+    peers(send_first)
+    for h in range(PARTS):
+        fill_first(h, me)
+    each(lambda d: stage1(1, d, d).wait_recv())
+    for h in range(PARTS):
+        def send_rest(d, h=h):
+            fill_rest(h, d)
+            stage2(h, 1, d, me).start()
+        peers(send_rest)
+        fill_rest(h, me)
+        self2(h).start()
 
     def invert(d, inv):
         for j in range(all_cols):
@@ -305,7 +317,7 @@
         def step(t, inner):
             prepare(h, t)
             return inner
-        lax.fori_loop(0, tiles, step, 0)
+        lax.fori_loop(0, tiles, step, 0, unroll=6)
 
         def first(base, rows):
             for f, value in enumerate(increments(h, 1, base, rows)):
@@ -362,8 +374,9 @@
     def take(h, sender):
         @pl.when(sender != me)
         def _():
-            for c in range(2):
-                stage2(h, c, sender, sender).wait_recv()
+            if h == 0:
+                stage2(0, 0, sender, sender).wait_recv()
+            stage2(h, 1, sender, sender).wait_recv()
 
         @pl.when(sender == me)
         def _():
@@ -481,10 +494,11 @@
 
     def drain(d):
         planmsg(d, me).wait_send()
+        stage2(0, 0, d, me).wait_send()
+        for h in range(PARTS):
+            stage2(h, 1, d, me).wait_send()
         for c in range(2):
             stage1(c, d, me).wait_send()
-            for h in range(PARTS):
-                stage2(h, c, d, me).wait_send()
         for c in range(2):
             for h in range(PARTS):
                 back1(h, c, d, me).wait_send()

time: 49 us -> 48.5 us (0.990)
  Pallas kernels: 48.2 us -> 47.7 us
where the time goes in v5:
time: 48.5 us; the launch traced here: 48.4 us
  Pallas kernels  47.7 us (98%)
  between operations  0.64 us (1%)
    pallas_call x1, Pallas kernels, body(): pl.pallas_call(functools.partial(kernel, n_lon, n_lat), out_shape=tuple((...  46.6 us
    pallas_call x1, Pallas kernels, body(): pl.pallas_call(hand_over, out_shape=tuple((jax.ShapeDtypeStruct(s, f32) f...  1.12 us

profile of v5, /device:TPU:0, one launch (start us, length us, event | category | flops | bytes accessed | tf_op | source)
XLA Modules:
  0.0 48.4 jit_solution(4051745395286534663)
XLA Ops:
  0.6 46.6 %shard_map.85 = (f32[2,128,512]{2,1,0:T(8,128)S(1)}, f32[2,128,512]{2,1,0:T(8,128)S(1)}, f32[1,2,3,128,128]{4,3,2,1,0:T(8,128)S(1)}) custom-call(s32[1,4]{1,0:T(1,128)} %plan_ref.1, f32[2,128,512]{2,1,0:T(8,128)} %vel_ref.1, f32[2,128,512]{2,1,0:T(8,128)} %frc_ref.1, f32[128,512]{1,0:T(8,128)} %str_ref.1, f32[128,512]{1,0:T(8,128)} %mob_ref.1, ...), custom_call_target="tpu_custom_call" | custom-call | tf_op jit(solution)/shard_map/pallas_call | solution.py:534
  47.3 1.1 %shard_map.86 = (f32[2,128,512]{2,1,0:T(8,128)}, f32[2,128,512]{2,1,0:T(8,128)}, f32[1,2,3,128,128]{4,3,2,1,0:T(8,128)}) custom-call(f32[2,128,512]{2,1,0:T(8,128)S(1)} %get-tuple-element.6.refs_0_, f32[2,128,512]{2,1,0:T(8,128)S(1)} %get-tuple-element.7.refs_1_, f32[1,2,3,128,128]{4,3,2,1,0:T(8,128)S(1)} %get-tuple-element.8.refs_2_), custom_call_target="tpu_custom_call" | custom-call | tf_op jit(solution)/shard_map/pallas_call | solution.py:575

commit v6 on v5

--- a/solution.py
+++ b/solution.py
@@ -132,7 +132,18 @@
         to(edge_l, halo_r, x_s.at[0], x_r.at[0], lon=left),
         to(edge_r, halo_l, x_s.at[1], x_r.at[1], lon=right),
     ]
+    y_copies = []
+    for i, span in enumerate((pl.ds(0, cols), pl.ds(cols, 1))):
+        y_copies += [
+            to(cst.at[:, :, span, pl.ds(TOP, HALO), :], cst.at[:, :, span, pl.ds(TOP + side, HALO), :],
+               y_s.at[2 * i], y_r.at[2 * i], lat=above),
+            to(cst.at[:, :, span, pl.ds(TOP + side - HALO, HALO), :],
+               cst.at[:, :, span, pl.ds(TOP - HALO, HALO), :],
+               y_s.at[2 * i + 1], y_r.at[2 * i + 1], lat=below),
+        ]
     for c in x_copies:
+        c.start()
+    for c in y_copies[:2]:
         c.start()
     each(lambda d: planmsg(d, me).start())
     for c in range(2):
@@ -148,31 +159,6 @@
         c.start()
     self_plan = pltpu.make_async_copy(plan_own, plan_all.at[me], one_sem.at[1])
     self_plan.start()
-
-    for c in x_copies:
-        c.wait_recv()
-    for f in range(7):
-        from_r, from_l = (
-            jnp.concatenate([got[...], pltpu.roll(got[...], LANES // 2, 1)], 0) for got in (halo_r, halo_l)
-        )
-        if f:
-            from_r = pltpu.roll(from_r, LANES - HALO * f, 1)
-            from_l = pltpu.roll(from_l, HALO * f, 1)
-        for h in range(PARTS):
-            a = from_r if h == PARTS - 1 else cst[h + 1, f, 0, own_rows, :]
-            b = from_l if h == 0 else cst[h - 1, f, cols - 1, own_rows, :]
-            cst[h, f, cols, own_rows, :] = jnp.where(
-                lane1 < HALO, a, jnp.where(lane1 >= LANES - HALO, b, 0.0)
-            )
-    y_copies = [
-        to(cst.at[:, :, :, pl.ds(TOP, HALO), :], cst.at[:, :, :, pl.ds(TOP + side, HALO), :],
-           y_s.at[0], y_r.at[0], lat=above),
-        to(cst.at[:, :, :, pl.ds(TOP + side - HALO, HALO), :],
-           cst.at[:, :, :, pl.ds(TOP - HALO, HALO), :],
-           y_s.at[1], y_r.at[1], lat=below),
-    ]
-    for c in y_copies:
-        c.start()
 
     each(lambda d: planmsg(d, d).wait_recv())
     self_plan.wait()
@@ -242,6 +228,24 @@
     peers(send_first)
     for h in range(PARTS):
         fill_first(h, me)
+    for c in x_copies:
+        c.wait_recv()
+    for f in range(7):
+        from_r, from_l = (
+            jnp.concatenate([got[...], pltpu.roll(got[...], LANES // 2, 1)], 0) for got in (halo_r, halo_l)
+        )
+        if f:
+            from_r = pltpu.roll(from_r, LANES - HALO * f, 1)
+            from_l = pltpu.roll(from_l, HALO * f, 1)
+        for h in range(PARTS):
+            a = from_r if h == PARTS - 1 else cst[h + 1, f, 0, own_rows, :]
+            b = from_l if h == 0 else cst[h - 1, f, cols - 1, own_rows, :]
+            cst[h, f, cols, own_rows, :] = jnp.where(
+                lane1 < HALO, a, jnp.where(lane1 >= LANES - HALO, b, 0.0)
+            )
+    for c in y_copies[2:]:
+        c.start()
+
     each(lambda d: stage1(1, d, d).wait_recv())
     for h in range(PARTS):
         def send_rest(d, h=h):
@@ -564,7 +568,7 @@
                 dma((2 * n_lon,)), dma((2 * n_lon,)),
                 dma((n_lon,)), dma((n_lon,)),
                 dma((2,)), dma((2,)),
-                dma((2,)), dma((2,)),
+                dma((4,)), dma((4,)),
                 dma((2 * PARTS * n_lon,)), dma((2 * PARTS * n_lon,)),
                 dma((2 * PARTS,)), dma((2 * PARTS,)),
                 dma((2 * PARTS * n_lon,)), dma((2 * PARTS * n_lon,)),

time: 48.5 us -> 48.2 us (level)
  no operation moved by 1% of the time
where the time goes in v6:
time: 48.2 us; the launch traced here: 48.1 us
  Pallas kernels  47.5 us (99%)
  between operations  0.64 us (1%)
    pallas_call x1, Pallas kernels, body(): pl.pallas_call(functools.partial(kernel, n_lon, n_lat), out_shape=tuple((...  46.3 us
    pallas_call x1, Pallas kernels, body(): pl.pallas_call(hand_over, out_shape=tuple((jax.ShapeDtypeStruct(s, f32) f...  1.12 us

profile of v6, /device:TPU:0, one launch (start us, length us, event | category | flops | bytes accessed | tf_op | source)
XLA Modules:
  0.0 48.1 jit_solution(13110670971945150134)
XLA Ops:
  0.6 46.3 %shard_map.85 = (f32[2,128,512]{2,1,0:T(8,128)S(1)}, f32[2,128,512]{2,1,0:T(8,128)S(1)}, f32[1,2,3,128,128]{4,3,2,1,0:T(8,128)S(1)}) custom-call(s32[1,4]{1,0:T(1,128)} %plan_ref.1, f32[2,128,512]{2,1,0:T(8,128)} %vel_ref.1, f32[2,128,512]{2,1,0:T(8,128)} %frc_ref.1, f32[128,512]{1,0:T(8,128)} %str_ref.1, f32[128,512]{1,0:T(8,128)} %mob_ref.1, ...), custom_call_target="tpu_custom_call" | custom-call | tf_op jit(solution)/shard_map/pallas_call | solution.py:538
  47.0 1.1 %shard_map.86 = (f32[2,128,512]{2,1,0:T(8,128)}, f32[2,128,512]{2,1,0:T(8,128)}, f32[1,2,3,128,128]{4,3,2,1,0:T(8,128)}) custom-call(f32[2,128,512]{2,1,0:T(8,128)S(1)} %get-tuple-element.6.refs_0_, f32[2,128,512]{2,1,0:T(8,128)S(1)} %get-tuple-element.7.refs_1_, f32[1,2,3,128,128]{4,3,2,1,0:T(8,128)S(1)} %get-tuple-element.8.refs_2_), custom_call_target="tpu_custom_call" | custom-call | tf_op jit(solution)/shard_map/pallas_call | solution.py:579

commit v7 on v6

--- a/solution.py
+++ b/solution.py
@@ -10,7 +10,7 @@
 NSUB = 4
 PARTS = 2
 FAR_FIRST = (10, 9, 11, 6, 14, 5, 15, 7, 13, 2, 8, 1, 3, 4, 12)
-DEPTH = 5
+DEPTH = 4
 DECAY = 0.8
 LANES = 128
 HALO = 8

time: 48.2 us -> 48.3 us (level)
  no operation moved by 1% of the time
where the time goes in v7:
time: 48.3 us; the launch traced here: 48.2 us
  Pallas kernels  47.5 us (98%)
  between operations  0.64 us (1%)
    pallas_call x1, Pallas kernels, body(): pl.pallas_call(functools.partial(kernel, n_lon, n_lat), out_shape=tuple((...  46.4 us
    pallas_call x1, Pallas kernels, body(): pl.pallas_call(hand_over, out_shape=tuple((jax.ShapeDtypeStruct(s, f32) f...  1.12 us

profile of v7, /device:TPU:0, one launch (start us, length us, event | category | flops | bytes accessed | tf_op | source)
XLA Modules:
  0.0 48.2 jit_solution(6675971839756364781)
XLA Ops:
  0.6 46.4 %shard_map.85 = (f32[2,128,512]{2,1,0:T(8,128)S(1)}, f32[2,128,512]{2,1,0:T(8,128)S(1)}, f32[1,2,3,128,128]{4,3,2,1,0:T(8,128)S(1)}) custom-call(s32[1,4]{1,0:T(1,128)} %plan_ref.1, f32[2,128,512]{2,1,0:T(8,128)} %vel_ref.1, f32[2,128,512]{2,1,0:T(8,128)} %frc_ref.1, f32[128,512]{1,0:T(8,128)} %str_ref.1, f32[128,512]{1,0:T(8,128)} %mob_ref.1, ...), custom_call_target="tpu_custom_call" | custom-call | tf_op jit(solution)/shard_map/pallas_call | solution.py:538
  47.1 1.1 %shard_map.86 = (f32[2,128,512]{2,1,0:T(8,128)}, f32[2,128,512]{2,1,0:T(8,128)}, f32[1,2,3,128,128]{4,3,2,1,0:T(8,128)}) custom-call(f32[2,128,512]{2,1,0:T(8,128)S(1)} %get-tuple-element.6.refs_0_, f32[2,128,512]{2,1,0:T(8,128)S(1)} %get-tuple-element.7.refs_1_, f32[1,2,3,128,128]{4,3,2,1,0:T(8,128)S(1)} %get-tuple-element.8.refs_2_), custom_call_target="tpu_custom_call" | custom-call | tf_op jit(solution)/shard_map/pallas_call | solution.py:579
